TPU v7x, 256 devices: a whole 4x4x8 slice. The times are simulated.
256 devices in a mesh: shock: 16 (over y, x_lo, core), trans: 16 (over z, x_hi).
Axes of the slice: x: 4 (x_hi: 2, x_lo: 2; x = x_hi * 2 + x_lo), y: 4, z: 8, core: 2. Of those that a mesh axis runs over, the one named last changes fastest.
Arguments:
- positions: float32 [32, 16, 3, 128], P('shock', 'trans'), may hold values from 0.35 to 12.8, as said below
- velocities: float32 [32, 16, 3, 128], P('shock', 'trans'), may hold values from -3 to 3
- features: bfloat16 [32, 16, 576, 128], P('shock', 'trans'), may hold values from -6 to 6
- neighbours: int32 [32, 16, 24, 128], P('shock', 'trans'), may hold values from 0 to 3455, as said below
- counts: int32 [32, 16, 128], P('shock', 'trans'), may hold values from 12 to 24, as said below
- w_first: float32 [64, 8], replicated, may hold values from -2 to 2
- w_second: float32 [192, 64], replicated, may hold values from -0.75 to 0.75
- w_read: float32 [128, 192], replicated, may hold values from -0.4375 to 0.4375
- w_out: float32 [128], replicated, may hold values from -0.5 to 0.5
- fresh_positions: float32 [16, 3, 128], P('trans'), may hold values from 0.35 to 12.8, as said below
- fresh_velocities: float32 [16, 3, 128], P('trans'), may hold values from -3 to 3
Outputs:
- energies: float32 [32, 16, 128], P('shock', 'trans')
- new_positions: float32 [32, 16, 3, 128], P('shock', 'trans')
- new_velocities: float32 [32, 16, 3, 128], P('shock', 'trans')
Inputs may be any that keep to these rules, and one draw needn't show every extreme that they name: `positions`: Block-local coordinates of each block's 128 atoms lie near the sites of a body-centred cubic arrangement of 4 x 4 x 4 cells of side 3.3 inside a cube of side 13.2. `fresh_positions`: as for positions. `neighbours`: each code is ((dz + 1) * 9 + (ds + 1) * 3 + (dt + 1)) * 128 + j with ds, dt, dz in -1 .. 1, naming a lattice neighbour of the atom other than itself at a distance between 1.2 and 8.8; codes of an atom are distinct. `counts`: slots at or beyond an atom's count are padding. Every atom of the block rows below 16 has all 24 slots live.
All inputs are finite; a program needn't handle non-finite values.
Results may differ from a plain program's by a relative error of at most 0.0006.
Values may be sent and summed in bfloat16 or wider, within the bound.
A program may use at most 128 MiB of HBM per device.

v0:
```python
import math

import jax
import jax.numpy as jnp
from jax import lax
from jax.sharding import PartitionSpec as P

CUTOFF_RADIUS = 9.5
BLOCK_LENGTH = 13.2
KICK_FACTOR = 4.0
MOVE_FACTOR = 0.5
HIGHEST_MODE = lax.Precision.HIGHEST


def extended_2(x, sides, width):
    for axis, dim in sides:
        count, length = (lax.axis_size(axis), x.shape[dim])
        up = [(i, (i + 1) % count) for i in range(count)]
        down = [(j, i) for i, j in up]
        last = lax.slice_in_dim(x, length - width, length, axis=dim)
        first = lax.slice_in_dim(x, 0, width, axis=dim)
        before = lax.ppermute(last, axis, up)
        after = lax.ppermute(first, axis, down)
        x = jnp.concatenate([before, x, after], axis=dim)
    return x


def shifted(x, axis, by):
    count = lax.axis_size(axis)
    return lax.ppermute(x, axis, [(i, (i + by) % count) for i in range(count)])


def passed_along(block, axis, distance):
    devices = range(lax.axis_size(axis))
    route = [(i - distance, i) for i in devices if i - distance in devices]
    return lax.ppermute(block, axis, route)


def block_energy(window_pos, window_feat, slot_codes, live_count, w_first, w_second, w_read, w_out):
    channels = w_second.shape[0] // 3
    basis_count = w_first.shape[1]
    neighbors = slot_codes.shape[0]
    window_slot = slot_codes % 1152
    image_z = (slot_codes // 1152 - 1).astype(jnp.float32)
    near_block = window_slot // 128
    shock_shift = (near_block // 3 - 1).astype(jnp.float32)
    trans_shift = (near_block % 3 - 1).astype(jnp.float32)
    offsets = jnp.stack([shock_shift, trans_shift, image_z]) * BLOCK_LENGTH
    centre = window_pos[:, 512:640]
    others = jnp.take(window_pos, window_slot, axis=1)
    displace = others + offsets - centre[:, None, :]
    distance = jnp.sqrt(jnp.sum(displace * displace, axis=0))
    heading = displace / distance[None]
    ratio = distance / CUTOFF_RADIUS
    envelope = 1.0 - 28.0 * ratio**6 + 48.0 * ratio**7 - 21.0 * ratio**8
    freqs = math.pi / CUTOFF_RADIUS * jnp.arange(1, basis_count + 1).astype(jnp.float32)
    basis = (
        math.sqrt(2.0 / CUTOFF_RADIUS)
        * jnp.sin(freqs[:, None, None] * distance[None])
        / distance[None]
    )
    slot_rank = lax.broadcasted_iota(jnp.int32, slot_codes.shape, 0)
    live = (slot_rank < live_count[None, :]).astype(jnp.float32)
    hidden = jax.nn.silu(jnp.dot(w_first, basis.reshape(basis_count, -1), precision=HIGHEST_MODE))
    radial = jnp.dot(w_second, hidden, precision=HIGHEST_MODE).reshape(3, channels, neighbors, 128)
    radial = radial * (envelope * live)[None, None]
    unit_x, unit_y, unit_z = (heading[0], heading[1], heading[2])
    root_three = math.sqrt(3.0)
    root_fifteen = math.sqrt(15.0)
    root_five = math.sqrt(5.0)
    harmonics = jnp.stack(
        [
            jnp.ones_like(unit_x),
            root_three * unit_x,
            root_three * unit_y,
            root_three * unit_z,
            root_fifteen * unit_x * unit_y,
            root_fifteen * unit_y * unit_z,
            0.5 * root_five * (3.0 * unit_z * unit_z - 1.0),
            root_fifteen * unit_x * unit_z,
            0.5 * root_fifteen * (unit_x * unit_x - unit_y * unit_y),
        ]
    )
    gathered = (
        jnp.take(window_feat, window_slot, axis=1)
        .reshape(9, channels, neighbors, 128)
        .astype(jnp.float32)
    )
    along = jnp.einsum("cna,mna->mca", radial[0] * gathered[0], harmonics, precision=HIGHEST_MODE)
    direct = jnp.sum(radial[1][None] * gathered, axis=2)
    vector_dot = jnp.sum(gathered[1:4] * harmonics[1:4][:, None], axis=0)
    coupled = jnp.sum(radial[2] * vector_dot, axis=1)
    tensor_sum = (along + direct).at[0].add(coupled) / neighbors
    squares = tensor_sum * tensor_sum
    invariants = jnp.concatenate(
        [squares[0], jnp.sum(squares[1:4], axis=0), jnp.sum(squares[4:9], axis=0)], axis=0
    )
    readout = jax.nn.silu(jnp.dot(w_read, invariants, precision=HIGHEST_MODE))
    return jnp.dot(w_out, readout, precision=HIGHEST_MODE)


def take_window(extended, row, col):
    zero = jnp.zeros((), jnp.int32)
    piece = lax.dynamic_slice(extended, (row, col, zero, zero), (3, 3, extended.shape[2], 128))
    return jnp.moveaxis(piece, 2, 0).reshape(extended.shape[2], 1152)


def sweep(pos_ext, feat_ext, neighbours, counts, w_first, w_second, w_read, w_out):
    nrows, ncols = (neighbours.shape[0], neighbours.shape[1])
    zero = jnp.zeros((), jnp.int32)

    def visit(block_id, carry):
        forces, energies = carry
        row = (block_id // ncols).astype(jnp.int32)
        col = (block_id % ncols).astype(jnp.int32)
        window_pos = take_window(pos_ext, row, col)
        window_feat = take_window(feat_ext, row, col)
        slot_codes = lax.dynamic_slice(
            neighbours, (row, col, zero, zero), (1, 1, neighbours.shape[2], 128)
        )[0, 0]
        live_count = lax.dynamic_slice(counts, (row, col, zero), (1, 1, 128))[0, 0]

        def energy_of(place):
            return block_energy(
                place, window_feat, slot_codes, live_count, w_first, w_second, w_read, w_out
            )

        energy, pullback = jax.vjp(energy_of, window_pos)
        grad = pullback(jnp.ones_like(energy))[0]
        piece = jnp.moveaxis(grad.reshape(3, 3, 3, 128), 0, 2)
        current = lax.dynamic_slice(forces, (row, col, zero, zero), (3, 3, 3, 128))
        forces = lax.dynamic_update_slice(forces, current - piece, (row, col, zero, zero))
        energies = lax.dynamic_update_slice(energies, energy[None, None], (row, col, zero))
        return (forces, energies)

    start = (jnp.zeros(pos_ext.shape, jnp.float32), jnp.zeros((nrows, ncols, 128), jnp.float32))
    return lax.fori_loop(0, nrows * ncols, visit, start)


def local(
    positions,
    velocities,
    features,
    neighbours,
    counts,
    w_first,
    w_second,
    w_read,
    w_out,
    fresh_positions,
    fresh_velocities,
):
    nrows, ncols = (positions.shape[0], positions.shape[1])
    shock_place = lax.axis_index("shock")
    front = lax.axis_size("shock") - 1
    pos_ext = extended_2(positions, (("shock", 0), ("trans", 1)), 1)
    feat_ext = extended_2(features, (("shock", 0), ("trans", 1)), 1)
    ext_rows = lax.broadcasted_iota(jnp.int32, (nrows + 2, 1, 1, 1), 0)
    outside = (ext_rows == 0) & (shock_place == 0) | (ext_rows == nrows + 1) & (
        shock_place == front
    )
    pos_ext = jnp.where(outside, jnp.zeros((), jnp.float32), pos_ext)
    feat_ext = jnp.where(outside, jnp.zeros((), jnp.bfloat16), feat_ext)
    forces_ext, energies = sweep(
        pos_ext, feat_ext, neighbours, counts, w_first, w_second, w_read, w_out
    )
    from_right = shifted(forces_ext[:, 0], "trans", -1)
    from_left = shifted(forces_ext[:, ncols + 1], "trans", 1)
    folded = forces_ext[:, 1 : ncols + 1]
    folded = folded.at[:, ncols - 1].add(from_right)
    folded = folded.at[:, 0].add(from_left)
    partial_force = folded[1 : nrows + 1]
    from_front = passed_along(folded[0], "shock", -1)
    from_rear = passed_along(folded[nrows + 1], "shock", 1)
    total_force = partial_force.at[nrows - 1].add(from_front)
    total_force = total_force.at[0].add(from_rear)
    new_vel = velocities + KICK_FACTOR * total_force
    moved = positions + MOVE_FACTOR * new_vel
    incoming_pos, incoming_vel = passed_along((moved[0], new_vel[0]), "shock", -1)
    kept_pos = moved[1:]
    kept_vel = new_vel[1:]
    at_front = shock_place == front
    last_pos = jnp.where(at_front, fresh_positions, incoming_pos)
    last_vel = jnp.where(at_front, fresh_velocities, incoming_vel)
    new_positions = jnp.concatenate([kept_pos, last_pos[None]], axis=0)
    new_velocities = jnp.concatenate([kept_vel, last_vel[None]], axis=0)
    return (energies, new_positions, new_velocities)


def solution(mesh):
    return jax.shard_map(
        local,
        mesh=mesh,
        in_specs=(
            P("shock", "trans", None, None),
            P("shock", "trans", None, None),
            P("shock", "trans", None, None),
            P("shock", "trans", None, None),
            P("shock", "trans", None),
            P(),
            P(),
            P(),
            P(),
            P("trans", None, None),
            P("trans", None, None),
        ),
        out_specs=(
            P("shock", "trans", None),
            P("shock", "trans", None, None),
            P("shock", "trans", None, None),
        ),
        check_vma=False,
    )
```

profile of v0, /device:TPU:1, one launch (start us, length us, event | category | flops | bytes accessed | tf_op | source)
XLA Modules:
  0.0 384.8 jit_solution(16589801530243505091)
XLA Ops:
  12.5 5.4 %collective-permute-start.7 = (bf16[4,1,576,128]{3,2,1,0:T(8,128)(2,1)S(1)}, bf16[4,1,576,128]{3,2,1,0:T(8,128)(2,1)S(1)}, u32[]{:S(2)}, u32[]{:S(2)}) collective-permute-start(bf16[4,1,576,128]{3,2,1,0:T(8,128)(2,1)S(1)} %constant_dynamic-update-slice_fusion.9), channel_id=1, source_target_pairs={{1,0},{2,1},{3,2},{4,3},{5,4},{6,5},{7,6},{8,7},{9,8},{10,9},{11,1... | collective-permute-start | bytes 1769480 | tf_op jit(solution)/shard_map/ppermute | solution.py:23
  20.9 15.7 %collective-permute-done = f32[1,1,3,128]{3,0,2,1:T(1,128)S(1)} collective-permute-done((f32[1,1,3,128]{3,0,2,1:T(1,128)S(1)}, f32[1,1,3,128]{3,0,2,1:T(1,128)S(1)}, u32[]{:S(2)}, u32[]{:S(2)}) %collective-permute-start) | collective-permute-done | bytes 1568 | tf_op jit(solution)/shard_map/ppermute | solution.py:22
  38.1 4.0 %collective-permute-start.2 = (f32[4,1,3,128]{3,0,2,1:T(4,128)S(1)}, f32[4,1,3,128]{3,0,2,1:T(4,128)S(1)}, u32[]{:S(2)}, u32[]{:S(2)}) collective-permute-start(f32[4,1,3,128]{3,0,2,1:T(4,128)S(1)} %pad_maximum_fusion.1), channel_id=1, source_target_pairs={{0,1},{1,2},{2,3},{3,4},{4,5},{5,6},{6,7},{7,8},{8,9},{9,10},{10,1... | collective-permute-start | bytes 18440 | tf_op jit(solution)/shard_map/ppermute | solution.py:22
  42.1 4.9 %collective-permute-start.3 = (f32[4,1,3,128]{3,0,2,1:T(4,128)S(1)}, f32[4,1,3,128]{3,0,2,1:T(4,128)S(1)}, u32[]{:S(2)}, u32[]{:S(2)}) collective-permute-start(f32[4,1,3,128]{3,0,2,1:T(4,128)S(1)} %pad_maximum_fusion.1), channel_id=1, source_target_pairs={{1,0},{2,1},{3,2},{4,3},{5,4},{6,5},{7,6},{8,7},{9,8},{10,9},{11,1... | collective-permute-start | bytes 18440 | tf_op jit(solution)/shard_map/ppermute | solution.py:23
  50.7 302.2 %while.23 = (s32[]{:T(128)}, f32[4,3,3,128]{3,0,2,1:T(4,128)}, f32[2,1,128]{2,1,0:T(1,128)}, s32[2,1,24,128]{3,2,1,0:T(8,128)}, f32[4,3,3,128]{3,0,2,1:T(4,128)}...) while((s32[]{:T(128)}, f32[4,3,3,128]{3,0,2,1:T(4,128)}, ...), condition=%wide.region_15.16_spmd, body=%wide.region_0.15_spmd.sunk | while | flops 1112283520 | bytes 188844736 | solution.py:137
  74.9 8.1 %gather_fusion = f32[3072,3]{1,0:T(8,128)S(1)} fusion(f32[3,1152]{0,1:T(8,128)S(1)} %bitcast.313, s32[3072]{0:T(1024)S(1)} %get-tuple-element.653), kind=kCustom, calls=%fused_computation.clone.1 | custom fusion | bytes 86016 | tf_op jit(solution)/shard_map/while/body/eval_jaxpr/jvp(jit(_take))/gather | solution.py:50
  91.6 13.5 %gather_fusion.1 = bf16[3072,576]{1,0:T(8,128)(2,1)} fusion(bf16[576,1152]{0,1:T(8,128)(2,1)S(1)} %bitcast.298, s32[3072]{0:T(1024)S(1)} %get-tuple-element.653), kind=kCustom, calls=%fused_computation.1.clone.1 | custom fusion | bytes 7090176 | tf_op jit(solution)/shard_map/while/body/eval_jaxpr/jvp(jit(_take))/gather | solution.py:85
  105.1 4.9 %copy.287 = bf16[24,128,576]{1,0,2:T(8,128)(2,1)S(1)} copy(bf16[24,128,576]{2,1,0:T(8,128)(2,1)} %bitcast.305) | data formatting | bytes 7077888 | tf_op jit(solution)/shard_map/while/body/eval_jaxpr/jvp(jit(_take))/gather | solution.py:85
  110.0 6.8 %copy.288 = bf16[9,64,24,128]{1,2,3,0:T(8,128)(2,1)} copy(bf16[9,64,24,128]{3,2,1,0:T(8,128)(2,1)S(1)} %bitcast.306) | data formatting | bytes 7077888 | tf_op jit(solution)/shard_map/while/body/eval_jaxpr/jvp(jit(_take))/gather | solution.py:85
  116.9 9.1 %fusion.169 = f32[9,64,24,128]{1,2,3,0:T(8,128)} fusion(bf16[9,64,24,128]{1,2,3,0:T(8,128)(2,1)} %copy.288, pred[24,128]{0,1:T(8,128)(4,1)S(1)} %copy.289), kind=kLoop, calls=%fused_computation.6.clone.1 | loop fusion | flops 3538944 | bytes 10619904 | tf_op jit(solution)/shard_map/while/body/eval_jaxpr/jvp()/convert_element_type | solution.py:87
  126.0 5.0 %multiply_reduce_fusion.17 = f32[64,24,128]{0,1,2:T(8,128)} fusion(f32[9,64,24,128]{1,2,3,0:T(8,128)} %fusion.169, f32[3,24,128]{1,2,0:T(8,128)S(1)} %copy-done.5), kind=kLoop, calls=%fused_computation.10.clone.1 | loop fusion | flops 983040 | bytes 3182592 | tf_op jit(solution)/shard_map/while/body/eval_jaxpr/jvp()/reduce_sum | solution.py:91
  145.7 6.3 %multiply_reduce_fusion.16 = f32[9,64,128]{1,2,0:T(8,128)} fusion(f32[64,24,128]{0,1,2:T(8,128)S(1)} %slice_bitcast_fusion.14, bf16[9,64,24,128]{1,2,3,0:T(8,128)(2,1)S(1)} %bitcast.300, pred[24,128]{0,1:T(8,128)(4,1)S(1)} %copy.289), kind=kLoop, calls=%fused_computation.4.clone.1 | loop fusion | flops 7004160 | bytes 4623360 | tf_op jit(solution)/shard_map/while/body/eval_jaxpr/jvp()/reduce_sum | solution.py:90
  152.5 3.8 fusion.170
  164.7 4.2 %fusion.176 = f32[1,64,24,128]{1,2,3,0:T(8,128)S(1)} fusion(f32[9,24,128]{1,0,2:T(8,128)S(1)} %copy.282, f32[9,64,24,128]{1,2,3,0:T(8,128)} %fusion.169, f32[9,64,128]{1,0,2:T(8,128)S(1)} %multiply_multiply_fusion.10), kind=kOutput, calls=%fused_computation.24.clone.1 | convolution fusion | flops 21430272 | bytes 1978368 | tf_op jit(solution)/shard_map/while/body/eval_jaxpr/transpose(jvp(cna,mna->mca))/dot_general | solution.py:89
  172.4 3.8 copy.295
  186.9 4.5 %fusion.172 = f32[128,9,24]{2,1,0:T(8,128)S(1)} fusion(f32[9,64,128]{1,0,2:T(8,128)S(1)} %multiply_multiply_fusion.10, f32[3,64,24,128]{1,2,3,0:T(8,128)} %copy-done, f32[9,64,24,128]{1,2,3,0:T(8,128)} %fusion.169), kind=kOutput, calls=%fused_computation.36.clone.1 | convolution fusion | flops 21430272 | bytes 3551232 | tf_op jit(solution)/shard_map/while/body/eval_jaxpr/transpose(jvp(cna,mna->mca))/dot_general | solution.py:89
  192.5 17.2 %scatter_fusion = f32[3,1152]{0,1:T(8,128)S(1)} fusion(f32[3,1152]{0,1:T(8,128)S(1)} %pad.265, s32[3072]{0:T(1024)S(1)} %copy-done.22, f32[3072,3]{1,0:T(8,128)S(1)} %bitcast.311), kind=kCustom, calls=%fused_computation.2.clone.1 | custom fusion | flops 9216 | bytes 122880 | tf_op jit(solution)/shard_map/while/body/eval_jaxpr/transpose(jvp(jit(_take)))/scatter-add | solution.py:50
  215.4 8.1 %gather_fusion = f32[3072,3]{1,0:T(8,128)S(1)} fusion(f32[3,1152]{0,1:T(8,128)S(1)} %bitcast.313, s32[3072]{0:T(1024)S(1)} %get-tuple-element.653), kind=kCustom, calls=%fused_computation.clone.1 | custom fusion | bytes 86016 | tf_op jit(solution)/shard_map/while/body/eval_jaxpr/jvp(jit(_take))/gather | solution.py:50
  232.0 13.5 %gather_fusion.1 = bf16[3072,576]{1,0:T(8,128)(2,1)} fusion(bf16[576,1152]{0,1:T(8,128)(2,1)S(1)} %bitcast.298, s32[3072]{0:T(1024)S(1)} %get-tuple-element.653), kind=kCustom, calls=%fused_computation.1.clone.1 | custom fusion | bytes 7090176 | tf_op jit(solution)/shard_map/while/body/eval_jaxpr/jvp(jit(_take))/gather | solution.py:85
  245.5 4.9 %copy.287 = bf16[24,128,576]{1,0,2:T(8,128)(2,1)S(1)} copy(bf16[24,128,576]{2,1,0:T(8,128)(2,1)} %bitcast.305) | data formatting | bytes 7077888 | tf_op jit(solution)/shard_map/while/body/eval_jaxpr/jvp(jit(_take))/gather | solution.py:85
  250.5 6.8 %copy.288 = bf16[9,64,24,128]{1,2,3,0:T(8,128)(2,1)} copy(bf16[9,64,24,128]{3,2,1,0:T(8,128)(2,1)S(1)} %bitcast.306) | data formatting | bytes 7077888 | tf_op jit(solution)/shard_map/while/body/eval_jaxpr/jvp(jit(_take))/gather | solution.py:85
  257.4 9.1 %fusion.169 = f32[9,64,24,128]{1,2,3,0:T(8,128)} fusion(bf16[9,64,24,128]{1,2,3,0:T(8,128)(2,1)} %copy.288, pred[24,128]{0,1:T(8,128)(4,1)S(1)} %copy.289), kind=kLoop, calls=%fused_computation.6.clone.1 | loop fusion | flops 3538944 | bytes 10619904 | tf_op jit(solution)/shard_map/while/body/eval_jaxpr/jvp()/convert_element_type | solution.py:87
  266.5 5.0 %multiply_reduce_fusion.17 = f32[64,24,128]{0,1,2:T(8,128)} fusion(f32[9,64,24,128]{1,2,3,0:T(8,128)} %fusion.169, f32[3,24,128]{1,2,0:T(8,128)S(1)} %copy-done.5), kind=kLoop, calls=%fused_computation.10.clone.1 | loop fusion | flops 983040 | bytes 3182592 | tf_op jit(solution)/shard_map/while/body/eval_jaxpr/jvp()/reduce_sum | solution.py:91
  286.1 6.3 %multiply_reduce_fusion.16 = f32[9,64,128]{1,2,0:T(8,128)} fusion(f32[64,24,128]{0,1,2:T(8,128)S(1)} %slice_bitcast_fusion.14, bf16[9,64,24,128]{1,2,3,0:T(8,128)(2,1)S(1)} %bitcast.300, pred[24,128]{0,1:T(8,128)(4,1)S(1)} %copy.289), kind=kLoop, calls=%fused_computation.4.clone.1 | loop fusion | flops 7004160 | bytes 4623360 | tf_op jit(solution)/shard_map/while/body/eval_jaxpr/jvp()/reduce_sum | solution.py:90
  293.0 3.8 fusion.170
  305.2 4.2 %fusion.176 = f32[1,64,24,128]{1,2,3,0:T(8,128)S(1)} fusion(f32[9,24,128]{1,0,2:T(8,128)S(1)} %copy.282, f32[9,64,24,128]{1,2,3,0:T(8,128)} %fusion.169, f32[9,64,128]{1,0,2:T(8,128)S(1)} %multiply_multiply_fusion.10), kind=kOutput, calls=%fused_computation.24.clone.1 | convolution fusion | flops 21430272 | bytes 1978368 | tf_op jit(solution)/shard_map/while/body/eval_jaxpr/transpose(jvp(cna,mna->mca))/dot_general | solution.py:89
  312.9 3.8 copy.295
  327.3 4.5 %fusion.172 = f32[128,9,24]{2,1,0:T(8,128)S(1)} fusion(f32[9,64,128]{1,0,2:T(8,128)S(1)} %multiply_multiply_fusion.10, f32[3,64,24,128]{1,2,3,0:T(8,128)} %copy-done, f32[9,64,24,128]{1,2,3,0:T(8,128)} %fusion.169), kind=kOutput, calls=%fused_computation.36.clone.1 | convolution fusion | flops 21430272 | bytes 3551232 | tf_op jit(solution)/shard_map/while/body/eval_jaxpr/transpose(jvp(cna,mna->mca))/dot_general | solution.py:89
  333.0 17.2 %scatter_fusion = f32[3,1152]{0,1:T(8,128)S(1)} fusion(f32[3,1152]{0,1:T(8,128)S(1)} %pad.265, s32[3072]{0:T(1024)S(1)} %copy-done.22, f32[3072,3]{1,0:T(8,128)S(1)} %bitcast.311), kind=kCustom, calls=%fused_computation.2.clone.1 | custom fusion | flops 9216 | bytes 122880 | tf_op jit(solution)/shard_map/while/body/eval_jaxpr/transpose(jvp(jit(_take)))/scatter-add | solution.py:50
  353.6 5.2 %collective-permute-start.8 = (f32[4,3,128]{2,0,1:T(4,128)S(1)}, f32[4,3,128]{2,0,1:T(4,128)S(1)}, u32[]{:S(2)}, u32[]{:S(2)}) collective-permute-start(f32[4,3,128]{2,0,1:T(4,128)S(1)} %get-tuple-element.541), channel_id=1, source_target_pairs={{0,15},{1,0},{2,1},{3,2},{4,3},{5,4},{6,5},{7,6},{8,7},{9,8},{10,9... | collective-permute-start | bytes 18440 | tf_op jit(solution)/shard_map/ppermute | solution.py:30
  359.6 5.3 %collective-permute-done.9 = f32[4,3,128]{2,0,1:T(4,128)S(1)} collective-permute-done((f32[4,3,128]{2,0,1:T(4,128)S(1)}, f32[4,3,128]{2,0,1:T(4,128)S(1)}, u32[]{:S(2)}, u32[]{:S(2)}) %collective-permute-start.9) | collective-permute-done | bytes 6176 | tf_op jit(solution)/shard_map/ppermute | solution.py:30
  365.6 7.4 %collective-permute-start.10 = (f32[1,3,128]{2,0,1:T(1,128)S(1)}, f32[1,3,128]{2,0,1:T(1,128)S(1)}, u32[]{:S(2)}, u32[]{:S(2)}) collective-permute-start(f32[1,3,128]{2,0,1:T(1,128)S(1)} %get-tuple-element.544), channel_id=1, source_target_pairs={{16,0},{32,16},{48,32},{64,48},{80,64},{96,80},{112,96},{128,112},... | collective-permute-start | bytes 4616 | tf_op jit(solution)/shard_map/ppermute | solution.py:36
  (369 shorter events, 138.7 us)
Async XLA Ops:
  1.6 4.8 %collective-permute-start.4 = (bf16[1,1,576,128]{3,2,1,0:T(8,128)(2,1)S(1)}, bf16[1,1,576,128]{3,2,1,0:T(8,128)(2,1)S(1)}, u32[]{:S(2)}, u32[]{:S(2)}) collective-permute-start(bf16[1,1,576,128]{3,2,1,0:T(8,128)(2,1)S(1)} %get-tuple-element.540), channel_id=1, source_target_pairs={{0,16},{16,32},{32,48},{48,64},{64,80},{80,96},{96,112},{112,128},... | collective-permute-start | bytes 442376 | tf_op jit(solution)/shard_map/ppermute | solution.py:22
  4.3 5.7 %collective-permute-start.5 = (bf16[1,1,576,128]{3,2,1,0:T(8,128)(2,1)S(1)}, bf16[1,1,576,128]{3,2,1,0:T(8,128)(2,1)S(1)}, u32[]{:S(2)}, u32[]{:S(2)}) collective-permute-start(bf16[1,1,576,128]{3,2,1,0:T(8,128)(2,1)S(1)} %get-tuple-element.539), channel_id=1, source_target_pairs={{16,0},{32,16},{48,32},{64,48},{80,64},{96,80},{112,96},{128,112},... | collective-permute-start | bytes 442376 | tf_op jit(solution)/shard_map/ppermute | solution.py:23
  10.0 38.6 %collective-permute-start.6 = (bf16[4,1,576,128]{3,2,1,0:T(8,128)(2,1)S(1)}, bf16[4,1,576,128]{3,2,1,0:T(8,128)(2,1)S(1)}, u32[]{:S(2)}, u32[]{:S(2)}) collective-permute-start(bf16[4,1,576,128]{3,2,1,0:T(8,128)(2,1)S(1)} %constant_dynamic-update-slice_fusion.9), channel_id=1, source_target_pairs={{0,1},{1,2},{2,3},{3,4},{4,5},{5,6},{6,7},{7,8},{8,9},{9,10},{10,1... | collective-permute-start | bytes 1769480 | tf_op jit(solution)/shard_map/ppermute | solution.py:22
  12.5 36.1 %collective-permute-start.7 = (bf16[4,1,576,128]{3,2,1,0:T(8,128)(2,1)S(1)}, bf16[4,1,576,128]{3,2,1,0:T(8,128)(2,1)S(1)}, u32[]{:S(2)}, u32[]{:S(2)}) collective-permute-start(bf16[4,1,576,128]{3,2,1,0:T(8,128)(2,1)S(1)} %constant_dynamic-update-slice_fusion.9), channel_id=1, source_target_pairs={{1,0},{2,1},{3,2},{4,3},{5,4},{6,5},{7,6},{8,7},{9,8},{10,9},{11,1... | collective-permute-start | bytes 1769480 | tf_op jit(solution)/shard_map/ppermute | solution.py:23
  18.6 18.0 %collective-permute-start = (f32[1,1,3,128]{3,0,2,1:T(1,128)S(1)}, f32[1,1,3,128]{3,0,2,1:T(1,128)S(1)}, u32[]{:S(2)}, u32[]{:S(2)}) collective-permute-start(f32[1,1,3,128]{3,0,2,1:T(1,128)S(1)} %get-tuple-element.549), channel_id=1, source_target_pairs={{0,16},{16,32},{32,48},{48,64},{64,80},{80,96},{96,112},{112,128},... | collective-permute-start | bytes 4616 | tf_op jit(solution)/shard_map/ppermute | solution.py:22
  18.6 19.5 %collective-permute-start.1 = (f32[1,1,3,128]{3,0,2,1:T(1,128)S(1)}, f32[1,1,3,128]{3,0,2,1:T(1,128)S(1)}, u32[]{:S(2)}, u32[]{:S(2)}) collective-permute-start(f32[1,1,3,128]{3,0,2,1:T(1,128)S(1)} %get-tuple-element.550), channel_id=1, source_target_pairs={{16,0},{32,16},{48,32},{64,48},{80,64},{96,80},{112,96},{128,112},... | collective-permute-start | bytes 4616 | tf_op jit(solution)/shard_map/ppermute | solution.py:23
  38.1 9.8 %collective-permute-start.2 = (f32[4,1,3,128]{3,0,2,1:T(4,128)S(1)}, f32[4,1,3,128]{3,0,2,1:T(4,128)S(1)}, u32[]{:S(2)}, u32[]{:S(2)}) collective-permute-start(f32[4,1,3,128]{3,0,2,1:T(4,128)S(1)} %pad_maximum_fusion.1), channel_id=1, source_target_pairs={{0,1},{1,2},{2,3},{3,4},{4,5},{5,6},{6,7},{7,8},{8,9},{9,10},{10,1... | collective-permute-start | bytes 18440 | tf_op jit(solution)/shard_map/ppermute | solution.py:22
  42.1 5.8 %collective-permute-start.3 = (f32[4,1,3,128]{3,0,2,1:T(4,128)S(1)}, f32[4,1,3,128]{3,0,2,1:T(4,128)S(1)}, u32[]{:S(2)}, u32[]{:S(2)}) collective-permute-start(f32[4,1,3,128]{3,0,2,1:T(4,128)S(1)} %pad_maximum_fusion.1), channel_id=1, source_target_pairs={{1,0},{2,1},{3,2},{4,3},{5,4},{6,5},{7,6},{8,7},{9,8},{10,9},{11,1... | collective-permute-start | bytes 18440 | tf_op jit(solution)/shard_map/ppermute | solution.py:23
  87.2 17.9 %copy-start.13 = (f32[24,128]{1,0:T(8,128)}, f32[24,128]{1,0:T(8,128)S(1)}, u32[]{:S(2)}) copy-start(f32[24,128]{1,0:T(8,128)S(1)} %get-tuple-element.656) | copy-start | bytes 36868 | tf_op jit(solution)/shard_map/while
  116.9 9.1 %copy-start.5 = (f32[3,24,128]{1,2,0:T(8,128)S(1)}, f32[3,24,128]{1,2,0:T(8,128)}, u32[]{:S(2)}) copy-start(f32[3,24,128]{1,2,0:T(8,128)} %copy.290) | copy-start | bytes 110596 | tf_op jit(solution)/shard_map/while
  142.2 9.7 %copy-start = (f32[3,64,24,128]{1,2,3,0:T(8,128)}, f32[3,64,24,128]{1,2,3,0:T(8,128)S(1)}, u32[]{:S(2)}) copy-start(f32[3,64,24,128]{1,2,3,0:T(8,128)S(1)} %broadcast_multiply_fusion.2) | copy-start | bytes 7077892 | tf_op jit(solution)/shard_map/while
  160.2 8.7 %slice-start.4 = ((s8[4718592]{0:T(1024)(128)(4,1)}), s8[4194304]{0:T(1024)(128)(4,1)S(1)}, s32[]{:S(2)}) async-start(s8[4718592]{0:T(1024)(128)(4,1)} %bitcast.303), calls=%async_computation.4 | async-start | bytes 8388608 | tf_op jit(solution)/shard_map/while
  161.8 7.1 %slice-start.5 = ((s8[4718592]{0:T(1024)(128)(4,1)}), s8[524288]{0:T(1024)(128)(4,1)S(1)}, s32[]{:S(2)}) async-start(s8[4718592]{0:T(1024)(128)(4,1)} %bitcast.303), calls=%async_computation.5 | async-start | bytes 1048576 | tf_op jit(solution)/shard_map/while
  191.3 18.4 %copy-start.16 = (f32[3,3,3,128]{3,0,2,1:T(4,128)S(1)}, f32[3,3,3,128]{3,0,2,1:T(4,128)}, u32[]{:S(2)}) copy-start(f32[3,3,3,128]{3,0,2,1:T(4,128)} %get-tuple-element.647) | copy-start | bytes 41476 | tf_op jit(solution)/shard_map/while
  191.6 20.0 %copy-start.19 = (f32[128,128]{0,1:T(8,128)S(1)}, f32[128,128]{0,1:T(8,128)}, u32[]{:S(2)}) copy-start(f32[128,128]{0,1:T(8,128)} %copy-done.18) | copy-start | bytes 196612 | tf_op jit(solution)/shard_map/while
  191.6 20.0 %copy-start.31 = (f32[128]{0:T(128)S(1)}, f32[128]{0:T(128)}, u32[]{:S(2)}) copy-start(f32[128]{0:T(128)} %get-tuple-element.713) | copy-start | bytes 1540 | tf_op jit(solution)/shard_map/while
  191.6 20.0 %copy-start.32 = (f32[2,1,128]{2,1,0:T(1,128)S(1)}, f32[2,1,128]{2,1,0:T(1,128)}, u32[]{:S(2)}) copy-start(f32[2,1,128]{2,1,0:T(1,128)} %get-tuple-element.692) | copy-start | bytes 3076 | tf_op jit(solution)/shard_map/while
  227.7 17.9 %copy-start.13 = (f32[24,128]{1,0:T(8,128)}, f32[24,128]{1,0:T(8,128)S(1)}, u32[]{:S(2)}) copy-start(f32[24,128]{1,0:T(8,128)S(1)} %get-tuple-element.656) | copy-start | bytes 36868 | tf_op jit(solution)/shard_map/while
  257.4 9.1 %copy-start.5 = (f32[3,24,128]{1,2,0:T(8,128)S(1)}, f32[3,24,128]{1,2,0:T(8,128)}, u32[]{:S(2)}) copy-start(f32[3,24,128]{1,2,0:T(8,128)} %copy.290) | copy-start | bytes 110596 | tf_op jit(solution)/shard_map/while
  282.6 9.7 %copy-start = (f32[3,64,24,128]{1,2,3,0:T(8,128)}, f32[3,64,24,128]{1,2,3,0:T(8,128)S(1)}, u32[]{:S(2)}) copy-start(f32[3,64,24,128]{1,2,3,0:T(8,128)S(1)} %broadcast_multiply_fusion.2) | copy-start | bytes 7077892 | tf_op jit(solution)/shard_map/while
  300.7 8.7 %slice-start.4 = ((s8[4718592]{0:T(1024)(128)(4,1)}), s8[4194304]{0:T(1024)(128)(4,1)S(1)}, s32[]{:S(2)}) async-start(s8[4718592]{0:T(1024)(128)(4,1)} %bitcast.303), calls=%async_computation.4 | async-start | bytes 8388608 | tf_op jit(solution)/shard_map/while
  302.2 7.1 %slice-start.5 = ((s8[4718592]{0:T(1024)(128)(4,1)}), s8[524288]{0:T(1024)(128)(4,1)S(1)}, s32[]{:S(2)}) async-start(s8[4718592]{0:T(1024)(128)(4,1)} %bitcast.303), calls=%async_computation.5 | async-start | bytes 1048576 | tf_op jit(solution)/shard_map/while
  331.8 18.4 %copy-start.16 = (f32[3,3,3,128]{3,0,2,1:T(4,128)S(1)}, f32[3,3,3,128]{3,0,2,1:T(4,128)}, u32[]{:S(2)}) copy-start(f32[3,3,3,128]{3,0,2,1:T(4,128)} %get-tuple-element.647) | copy-start | bytes 41476 | tf_op jit(solution)/shard_map/while
  332.1 20.0 %copy-start.19 = (f32[128,128]{0,1:T(8,128)S(1)}, f32[128,128]{0,1:T(8,128)}, u32[]{:S(2)}) copy-start(f32[128,128]{0,1:T(8,128)} %copy-done.18) | copy-start | bytes 196612 | tf_op jit(solution)/shard_map/while
  332.1 20.0 %copy-start.31 = (f32[128]{0:T(128)S(1)}, f32[128]{0:T(128)}, u32[]{:S(2)}) copy-start(f32[128]{0:T(128)} %get-tuple-element.713) | copy-start | bytes 1540 | tf_op jit(solution)/shard_map/while
  332.1 20.0 %copy-start.32 = (f32[2,1,128]{2,1,0:T(1,128)S(1)}, f32[2,1,128]{2,1,0:T(1,128)}, u32[]{:S(2)}) copy-start(f32[2,1,128]{2,1,0:T(1,128)} %get-tuple-element.692) | copy-start | bytes 3076 | tf_op jit(solution)/shard_map/while
  353.6 5.9 %collective-permute-start.8 = (f32[4,3,128]{2,0,1:T(4,128)S(1)}, f32[4,3,128]{2,0,1:T(4,128)S(1)}, u32[]{:S(2)}, u32[]{:S(2)}) collective-permute-start(f32[4,3,128]{2,0,1:T(4,128)S(1)} %get-tuple-element.541), channel_id=1, source_target_pairs={{0,15},{1,0},{2,1},{3,2},{4,3},{5,4},{6,5},{7,6},{8,7},{9,8},{10,9... | collective-permute-start | bytes 18440 | tf_op jit(solution)/shard_map/ppermute | solution.py:30
  358.8 6.1 %collective-permute-start.9 = (f32[4,3,128]{2,0,1:T(4,128)S(1)}, f32[4,3,128]{2,0,1:T(4,128)S(1)}, u32[]{:S(2)}, u32[]{:S(2)}) collective-permute-start(f32[4,3,128]{2,0,1:T(4,128)S(1)} %get-tuple-element.542), channel_id=1, source_target_pairs={{0,1},{1,2},{2,3},{3,4},{4,5},{5,6},{6,7},{7,8},{8,9},{9,10},{10,1... | collective-permute-start | bytes 18440 | tf_op jit(solution)/shard_map/ppermute | solution.py:30
  365.6 9.3 %collective-permute-start.10 = (f32[1,3,128]{2,0,1:T(1,128)S(1)}, f32[1,3,128]{2,0,1:T(1,128)S(1)}, u32[]{:S(2)}, u32[]{:S(2)}) collective-permute-start(f32[1,3,128]{2,0,1:T(1,128)S(1)} %get-tuple-element.544), channel_id=1, source_target_pairs={{16,0},{32,16},{48,32},{64,48},{80,64},{96,80},{112,96},{128,112},... | collective-permute-start | bytes 4616 | tf_op jit(solution)/shard_map/ppermute | solution.py:36
  373.0 3.1 collective-permute-start.11
  376.8 5.0 %collective-permute-start.12 = (f32[1,3,128]{2,0,1:T(1,128)S(1)}, f32[1,3,128]{2,0,1:T(1,128)S(1)}, u32[]{:S(2)}, u32[]{:S(2)}) collective-permute-start(f32[1,3,128]{2,0,1:T(1,128)S(1)} %get-tuple-element.548), channel_id=1, source_target_pairs={{16,0},{32,16},{48,32},{64,48},{80,64},{96,80},{112,96},{128,112},... | collective-permute-start | bytes 4616 | tf_op jit(solution)/shard_map/ppermute | solution.py:36
  378.9 4.9 %collective-permute-start.13 = (f32[1,3,128]{2,0,1:T(1,128)S(1)}, f32[1,3,128]{2,0,1:T(1,128)S(1)}, u32[]{:S(2)}, u32[]{:S(2)}) collective-permute-start(f32[1,3,128]{2,0,1:T(1,128)S(1)} %get-tuple-element.546), channel_id=1, source_target_pairs={{16,0},{32,16},{48,32},{64,48},{80,64},{96,80},{112,96},{128,112},... | collective-permute-start | bytes 4616 | tf_op jit(solution)/shard_map/ppermute | solution.py:36
  (62 other events, 247.0 us)
where the time goes:
time: 392 us; the launch traced here: 385 us
  local copies, waits for them, and re-layouts  124 us (32%)
  other arithmetic  122 us (31%)
  matrix products  42.8 us (11%)
  starting transfers between devices  40.2 us (10%)
  waiting for transfers between devices  31.6 us (8%)
  loops' own time  22.8 us (6%)
    gather x6, local copies, waits for them, and re-layouts, block_energy(): jnp.take(window_feat, window_slot, axis=1)  50.4 us
    scatter-add x2, other arithmetic, block_energy(): others = jnp.take(window_pos, window_slot, axis=1)  34.3 us
    dot_general x6, matrix products, block_energy(): jnp.einsum('cna,mna->mca', radial[0] * gathered[0], harmonics, precision=...  24.9 us
    another operation x1, loops' own time, sweep(): return lax.fori_loop(0, nrows * ncols, visit, start)  22.8 us
    reduce_sum x4, other arithmetic, block_energy(): direct = jnp.sum(radial[1][None] * gathered, axis=2)  18.3 us
    convert_element_type x2, other arithmetic, block_energy(): gathered = jnp.take(window_feat, window_slot, axis=1).reshape(9, channels...  18.2 us
    ppermute x4, waiting for transfers between devices, extended_2(): before = lax.ppermute(last, axis, up)  18 us
    reduce_sum x4, other arithmetic, block_energy(): vector_dot = jnp.sum(gathered[1:4] * harmonics[1:4][:, None], axis=0)  17.7 us
  transfers between devices with their start and end apart: 14, of which 10 were waited for; matrix products, arithmetic and copies ran while one was open for 1% of the time, Pallas kernels for 0%

commit v1 on v0

v1 whole, which is shorter than its diff:
```python
import math

import jax
import jax.numpy as jnp
from jax import lax
from jax.experimental import pallas as pl
from jax.experimental.pallas import tpu as pltpu

CUTOFF_RADIUS = 9.5
BLOCK_LENGTH = 13.2
KICK_FACTOR = 4.0
MOVE_FACTOR = 0.5
F32 = jnp.float32
BF16 = jnp.bfloat16
GEO = 12
SPAN = 4


def split(x):
    hi = x.astype(BF16)
    return hi, (x - hi.astype(F32)).astype(BF16)


def sigmoid(z):
    return 0.5 * jnp.tanh(0.5 * z) + 0.5


def sin_cos_pi(t):
    whole = jnp.floor(t + 0.5)
    half = whole * 0.5
    sign = 1.0 - 4.0 * (half - jnp.floor(half))
    r = (t - whole) * math.pi
    r2 = r * r
    s = r * (1.0 + r2 * (-1 / 6 + r2 * (1 / 120 + r2 * (-1 / 5040 + r2 * (1 / 362880 - r2 / 39916800)))))
    c = 1.0 + r2 * (
        -1 / 2 + r2 * (1 / 24 + r2 * (-1 / 720 + r2 * (1 / 40320 + r2 * (-1 / 3628800 + r2 / 479001600))))
    )
    return s * sign, c * sign


def geometry(r, pos, codes, counts, geo, unit):
    for part in range(3):
        rows = slice(8 * part, 8 * part + 8)
        code = codes[r, 0, rows, :]
        j = code & 127
        cell = code >> 7
        iz = (cell >= 9).astype(jnp.int32) + (cell >= 18).astype(jnp.int32)
        k = cell - 9 * iz
        is_ = (k >= 3).astype(jnp.int32) + (k >= 6).astype(jnp.int32)
        it = k - 3 * is_
        shifts = [(v - 1).astype(F32) * BLOCK_LENGTH for v in (is_, it, iz)]
        delta = []
        for comp in range(3):
            other = jnp.zeros((8, 128), F32)
            for b in range(9):
                row = pos[r + b // 3, b % 3, pl.ds(comp, 8, stride=0), :]
                got = jnp.take_along_axis(row, j, axis=1, mode="promise_in_bounds")
                other = jnp.where(k == b, got, other)
            centre = pos[r + 1, 1, pl.ds(comp, 8, stride=0), :]
            delta.append(other + shifts[comp] - centre)
        dx, dy, dz = delta
        d = jnp.sqrt(dx * dx + dy * dy + dz * dz)
        rinv = 1.0 / d
        ux, uy, uz = dx * rinv, dy * rinv, dz * rinv
        x = d * (1.0 / CUTOFF_RADIUS)
        x2 = x * x
        x4 = x2 * x2
        slot = lax.broadcasted_iota(jnp.int32, (8, 128), 0) + 8 * part
        live = jnp.where(slot < counts[pl.ds(r, 8, stride=0), :], 1.0 / 24.0, 0.0)
        env = (1.0 + x4 * x2 * (-28.0 + x * (48.0 - 21.0 * x))) * live
        slope = (-168.0 / CUTOFF_RADIUS) * x4 * x * ((1.0 - x) * (1.0 - x)) * live
        r3, r5, r15 = math.sqrt(3.0), math.sqrt(5.0), math.sqrt(15.0)
        values = [
            r3 * ux,
            r3 * uy,
            r3 * uz,
            r15 * ux * uy,
            r15 * uy * uz,
            0.5 * r5 * (3.0 * uz * uz - 1.0),
            r15 * ux * uz,
            0.5 * r15 * (ux * ux - uy * uy),
            x,
            rinv,
            env,
            slope,
        ]
        for q, v in enumerate(values):
            geo[r, q, rows, :] = v
        for q, v in enumerate((ux, uy, uz)):
            unit[r, q, rows, :] = v


def radial(step, geo, first, second, basis, hid, wgt):
    per = 24 // SPAN
    r = step // per
    n0 = (step % per) * SPAN
    order = (lax.broadcasted_iota(jnp.int32, (8, 128), 0) + 1).astype(F32)
    scale = math.sqrt(2.0 / CUTOFF_RADIUS)
    zero8 = jnp.zeros((8, 128), F32)
    for q in range(SPAN):
        x = geo[r, 8, pl.ds(n0 + q, 8, stride=0), :]
        rinv = geo[r, 9, pl.ds(n0 + q, 8, stride=0), :]
        s, c = sin_cos_pi(x * order)
        b = (scale * rinv) * s
        bd = rinv * ((scale * math.pi / CUTOFF_RADIUS) * order * c - b)
        for v, at in ((b, q), (bd, SPAN + q)):
            hi = v.astype(BF16).astype(F32)
            lanes = slice(128 * at, 128 * at + 128)
            basis[0:16, lanes] = jnp.concatenate([hi, v - hi], axis=0).astype(BF16)
            basis[16:32, lanes] = jnp.concatenate([hi, zero8], axis=0).astype(BF16)
    z = jnp.dot(first, basis[...], preferred_element_type=F32)
    for q in range(SPAN):
        env = geo[r, 10, pl.ds(n0 + q, 8, stride=0), :]
        slope = geo[r, 11, pl.ds(n0 + q, 8, stride=0), :]
        env, slope = (jnp.concatenate([v] * 8, axis=0) for v in (env, slope))
        zq = z[:, 128 * q : 128 * q + 128]
        zd = z[:, 128 * (SPAN + q) : 128 * (SPAN + q) + 128]
        sig = sigmoid(zq)
        act = zq * sig
        h = act * env
        hd = (sig + act * (1.0 - sig)) * zd * env + act * slope
        for v, at in ((h, q), (hd, SPAN + q)):
            hi, lo = split(v)
            lanes = slice(128 * at, 128 * at + 128)
            hid[0:64, lanes] = hi
            hid[64:128, lanes] = lo
            hid[128:192, lanes] = hi
    w = jnp.dot(second, hid[...], preferred_element_type=F32)
    for q in range(SPAN):
        wgt[r, n0 + q, 0] = w[:, 128 * q : 128 * q + 128]
        wgt[r, n0 + q, 1] = w[:, 128 * (SPAN + q) : 128 * (SPAN + q) + 128]


def gather(step, codes, window, got):
    r = step // 12
    n0 = (step % 12) * 2
    ids = lax.broadcasted_iota(jnp.int32, (128, 128), 0).astype(F32).astype(BF16)
    halves = []
    for q in range(2):
        code = codes[r, 0, pl.ds(n0 + q, 16, stride=0), :]
        j = (code & 127).astype(F32)
        cell = code >> 7
        k = cell - 9 * ((cell >= 9).astype(jnp.int32) + (cell >= 18).astype(jnp.int32))
        pieces = []
        for b in range(9):
            val = jnp.where(k == b, j, -1.0).astype(BF16)
            val = jnp.concatenate([val] * 8, axis=0)
            pieces.append(jnp.where(val == ids, jnp.ones((), BF16), jnp.zeros((), BF16)))
        halves.append(jnp.concatenate(pieces, axis=0))
    hot = jnp.concatenate(halves, axis=1)
    out = jnp.dot(window[r], hot, preferred_element_type=F32)
    got[r, n0] = out[:, :128]
    got[r, n0 + 1] = out[:, 128:]


def row8(ref, r, q, n, times=1):
    v = ref[r, q, pl.ds(n, 8, stride=0), :]
    return v if times == 1 else jnp.concatenate([v] * times, axis=0)


TILE = 16


def aggregate(step, geo, wgt, got, agg):
    per = 64 // TILE
    r = step // per
    c0 = pl.multiple_of((step % per) * TILE, TILE)

    def body(n, acc):
        acc = list(acc)
        y = [None] + [row8(geo, r, q, n, TILE // 8) for q in range(8)]
        x = [got[r, n, pl.ds(m * 64 + c0, TILE), :] for m in range(9)]
        w = [wgt[r, n, 0, pl.ds(p * 64 + c0, TILE), :] for p in range(3)]
        p0 = w[0] * x[0]
        v = x[1] * y[1] + x[2] * y[2] + x[3] * y[3]
        acc[0] += p0 + w[1] * x[0] + w[2] * v
        for m in range(1, 9):
            acc[m] += p0 * y[m] + w[1] * x[m]
        return tuple(acc)

    acc = lax.fori_loop(0, 24, body, (jnp.zeros((TILE, 128), F32),) * 9, unroll=4)
    for m in range(9):
        agg[r, m, pl.ds(c0, TILE), :] = acc[m]


def readout(agg, read3, read_t3, w_out, energies):
    inv = []
    for r in range(2):
        a = [agg[r, m] for m in range(9)]
        sq = [v * v for v in a]
        inv.append(
            jnp.concatenate(
                [sq[0], sq[1] + sq[2] + sq[3], sq[4] + sq[5] + sq[6] + sq[7] + sq[8]], axis=0
            )
        )
    s = jnp.concatenate(inv, axis=1)
    hi, lo = split(s)
    z = jnp.dot(read3, jnp.concatenate([hi, lo, hi], axis=0), preferred_element_type=F32)
    sig = sigmoid(z)
    act = z * sig
    energy = jnp.sum(w_out * act, axis=0, keepdims=True)
    energies[0:1, :] = energy[:, :128]
    energies[1:2, :] = energy[:, 128:]
    gz = w_out * (sig + act * (1.0 - sig))
    hi, lo = split(gz)
    gs = jnp.dot(read_t3, jnp.concatenate([hi, lo, hi], axis=0), preferred_element_type=F32)
    gs = gs + gs
    for r in range(2):
        g = gs[:, 128 * r : 128 * r + 128]
        for m in range(9):
            part = 0 if m == 0 else 1 if m < 4 else 2
            agg[r, m] = agg[r, m] * g[64 * part : 64 * part + 64]


def backward(step, geo, wgt, got, agg, slopes):
    r = step // 24
    n = step % 24
    y = [None] + [row8(geo, r, q, n) for q in range(8)]
    acc = [jnp.zeros((8, 128), F32)] * 9
    for c in range(8):
        x = [got[r, n, m * 64 + 8 * c : m * 64 + 8 * c + 8, :] for m in range(9)]
        g = [agg[r, m, 8 * c : 8 * c + 8, :] for m in range(9)]
        w0, _, w2 = [wgt[r, n, 0, p * 64 + 8 * c : p * 64 + 8 * c + 8, :] for p in range(3)]
        d0, d1, d2 = [wgt[r, n, 1, p * 64 + 8 * c : p * 64 + 8 * c + 8, :] for p in range(3)]
        gx = g[0] * x[0]
        gy = g[0]
        for m in range(1, 9):
            gx += g[m] * x[m]
            gy += g[m] * y[m]
        v = x[1] * y[1] + x[2] * y[2] + x[3] * y[3]
        acc[0] += d1 * gx + d0 * (gy * x[0]) + d2 * (g[0] * v)
        p0 = w0 * x[0]
        p2 = w2 * g[0]
        for m in range(1, 9):
            acc[m] += p0 * g[m] + p2 * x[m] if m < 4 else p0 * g[m]
    for q in range(9):
        slopes[r, q, pl.ds(n, 1), :] = jnp.sum(acc[q], axis=0, keepdims=True)


def edge_forces(r, geo, unit, slopes, edge):
    r3, r5, r15 = math.sqrt(3.0), math.sqrt(5.0), math.sqrt(15.0)
    ux, uy, uz = (unit[r, q] for q in range(3))
    rinv = geo[r, 9]
    gd, g1, g2, g3, g4, g5, g6, g7, g8 = (slopes[r, q] for q in range(9))
    gx = r3 * g1 + r15 * (uy * g4 + uz * g7 + ux * g8)
    gy = r3 * g2 + r15 * (ux * g4 + uz * g5 - uy * g8)
    gz = r3 * g3 + r15 * (uy * g5 + ux * g7) + (3.0 * r5) * uz * g6
    along = gd - (gx * ux + gy * uy + gz * uz) * rinv
    out = []
    for q, (g, u) in enumerate(((gx, ux), (gy, uy), (gz, uz))):
        f = g * rinv + along * u
        edge[q] = f
        out.append(jnp.sum(f, axis=0, keepdims=True))
    return out


def scatter(r, codes, edge, lhs, hot, centre, forces):
    ids = lax.broadcasted_iota(jnp.int32, (128, 128), 0).astype(F32).astype(BF16)
    pick = lax.broadcasted_iota(jnp.int32, (8, 128), 0)

    def body(n, carry):
        code = codes[r, 0, pl.ds(n, 8, stride=0), :]
        cell = code >> 7
        k = cell - 9 * ((cell >= 9).astype(jnp.int32) + (cell >= 18).astype(jnp.int32))
        value = jnp.zeros((8, 128), F32)
        for q in range(3):
            f = edge[q, pl.ds(n, 8, stride=0), :]
            hi = f.astype(BF16).astype(F32)
            value = jnp.where(pick == q, hi, jnp.where(pick == q + 3, f - hi, value))
        rows = [jnp.where(k == b, value, 0.0) for b in range(9)] + [jnp.zeros((8, 128), F32)]
        lanes = pl.ds(pl.multiple_of(n * 128, 128), 128)
        lhs[:, lanes] = jnp.concatenate(rows, axis=0).astype(BF16)
        j = (codes[r, 0, pl.ds(n, 16, stride=0), :] & 127).astype(F32).astype(BF16)
        j = jnp.concatenate([j] * 8, axis=0)
        hot[:, lanes] = jnp.where(j == ids, jnp.ones((), BF16), jnp.zeros((), BF16))
        return carry

    lax.fori_loop(0, 24, body, 0, unroll=2)
    out = lax.dot_general(lhs[...], hot[...], (((1,), (1,)), ((), ())), preferred_element_type=F32)
    for b in range(9):
        at = (r + b // 3, b % 3)
        for q in range(3):
            v = -(out[8 * b + q : 8 * b + q + 1] + out[8 * b + q + 3 : 8 * b + q + 4])
            if b == 4:
                v += centre[q]
            forces[at[0], at[1], q : q + 1, :] += v


def split_whole(w):
    rounded = lax.reduce_precision(w, 8, 7)
    return rounded.astype(BF16), (w - rounded).astype(BF16)


def stack3(w):
    hi, lo = split_whole(w)
    return jnp.concatenate([hi, hi, lo], axis=1)


def block_kernel(
    pos, feat, codes, counts, w_first, w_second, w_read, w_read_t, w_out, energies, forces,
    geo, unit, basis, hid, wgt, window, got, agg, slopes, edge, lhs, hot,
):
    for r in range(2):
        geometry(r, pos, codes, counts, geo, unit)
        for b in range(9):
            window[r, :, 128 * b : 128 * b + 128] = feat[r + b // 3, b % 3]

    def radial_step(step, carry):
        radial(step, geo, w_first[...], w_second[...], basis, hid, wgt)
        return carry

    lax.fori_loop(0, 48 // SPAN, radial_step, 0)

    def gather_step(step, carry):
        gather(step, codes, window, got)
        return carry

    lax.fori_loop(0, 24, gather_step, 0)

    def aggregate_step(step, carry):
        aggregate(step, geo, wgt, got, agg)
        return carry

    lax.fori_loop(0, 2 * (64 // TILE), aggregate_step, 0)
    readout(agg, w_read[...], w_read_t[...], w_out[...], energies)

    def backward_step(step, carry):
        backward(step, geo, wgt, got, agg, slopes)
        return carry

    lax.fori_loop(0, 48, backward_step, 0)
    forces[...] = jnp.zeros_like(forces)
    for r in range(2):
        centre = edge_forces(r, geo, unit, slopes, edge)
        scatter(r, codes, edge, lhs, hot, centre, forces)


def weights(w_first, w_second, w_read, w_out):
    hi, lo = split_whole(w_first)
    first = jnp.concatenate([hi, hi, lo, jnp.zeros_like(hi)], axis=1)
    out = jnp.broadcast_to(w_out[:, None], (w_out.shape[0], 256))
    return first, stack3(w_second), stack3(w_read), stack3(w_read.T), out


def blocks(pos_ext, feat_ext, codes, counts, w):
    vmem = pl.BlockSpec(memory_space=pltpu.VMEM)
    return pl.pallas_call(
        block_kernel,
        out_shape=(
            jax.ShapeDtypeStruct((2, 128), F32),
            jax.ShapeDtypeStruct((4, 3, 3, 128), F32),
        ),
        in_specs=[vmem] * 9,
        out_specs=(vmem, vmem),
        scratch_shapes=[
            pltpu.VMEM((2, GEO, 24, 128), F32),
            pltpu.VMEM((2, 3, 24, 128), F32),
            pltpu.VMEM((32, 256 * SPAN), BF16),
            pltpu.VMEM((192, 256 * SPAN), BF16),
            pltpu.VMEM((2, 24, 2, 192, 128), F32),
            pltpu.VMEM((2, 576, 1152), BF16),
            pltpu.VMEM((2, 24, 576, 128), F32),
            pltpu.VMEM((2, 9, 64, 128), F32),
            pltpu.VMEM((2, 9, 24, 128), F32),
            pltpu.VMEM((3, 24, 128), F32),
            pltpu.VMEM((80, 3072), BF16),
            pltpu.VMEM((128, 3072), BF16),
        ],
        compiler_params=pltpu.CompilerParams(vmem_limit_bytes=56 << 20),
        name="blocks",
    )(pos_ext, feat_ext, codes, counts, *w)
from jax.sharding import PartitionSpec as P


def extended_2(x, sides, width):
    for axis, dim in sides:
        count, length = (lax.axis_size(axis), x.shape[dim])
        up = [(i, (i + 1) % count) for i in range(count)]
        down = [(j, i) for i, j in up]
        last = lax.slice_in_dim(x, length - width, length, axis=dim)
        first = lax.slice_in_dim(x, 0, width, axis=dim)
        before = lax.ppermute(last, axis, up)
        after = lax.ppermute(first, axis, down)
        x = jnp.concatenate([before, x, after], axis=dim)
    return x


def shifted(x, axis, by):
    count = lax.axis_size(axis)
    return lax.ppermute(x, axis, [(i, (i + by) % count) for i in range(count)])


def passed_along(block, axis, distance):
    devices = range(lax.axis_size(axis))
    route = [(i - distance, i) for i in devices if i - distance in devices]
    return lax.ppermute(block, axis, route)


def local(
    positions, velocities, features, neighbours, counts, w_first, w_second, w_read, w_out,
    fresh_positions, fresh_velocities,
):
    nrows, ncols = (positions.shape[0], positions.shape[1])
    shock_place = lax.axis_index("shock")
    front = lax.axis_size("shock") - 1
    pos_ext = extended_2(positions, (("trans", 1), ("shock", 0)), 1)
    feat_ext = extended_2(features, (("trans", 1), ("shock", 0)), 1)
    ext_rows = lax.broadcasted_iota(jnp.int32, (nrows + 2, 1, 1, 1), 0)
    outside = (ext_rows == 0) & (shock_place == 0) | (ext_rows == nrows + 1) & (
        shock_place == front
    )
    pos_ext = jnp.where(outside, jnp.zeros((), jnp.float32), pos_ext)
    feat_ext = jnp.where(outside, jnp.zeros((), jnp.bfloat16), feat_ext)
    energies, forces_ext = blocks(
        pos_ext, feat_ext, neighbours, counts[:, 0], weights(w_first, w_second, w_read, w_out)
    )
    from_right = shifted(forces_ext[:, 0], "trans", -1)
    from_left = shifted(forces_ext[:, ncols + 1], "trans", 1)
    folded = forces_ext[:, 1 : ncols + 1]
    folded = folded.at[:, ncols - 1].add(from_right)
    folded = folded.at[:, 0].add(from_left)
    partial_force = folded[1 : nrows + 1]
    from_front = passed_along(folded[0], "shock", -1)
    from_rear = passed_along(folded[nrows + 1], "shock", 1)
    total_force = partial_force.at[nrows - 1].add(from_front)
    total_force = total_force.at[0].add(from_rear)
    new_vel = velocities + KICK_FACTOR * total_force
    moved = positions + MOVE_FACTOR * new_vel
    incoming_pos, incoming_vel = passed_along((moved[0], new_vel[0]), "shock", -1)
    at_front = shock_place == front
    last_pos = jnp.where(at_front, fresh_positions, incoming_pos)
    last_vel = jnp.where(at_front, fresh_velocities, incoming_vel)
    new_positions = jnp.concatenate([moved[1:], last_pos[None]], axis=0)
    new_velocities = jnp.concatenate([new_vel[1:], last_vel[None]], axis=0)
    return (energies[:, None], new_positions, new_velocities)


def solution(mesh):
    spec = P("shock", "trans", None, None)
    return jax.shard_map(
        local,
        mesh=mesh,
        in_specs=(
            spec, spec, spec, spec, P("shock", "trans", None), P(), P(), P(), P(),
            P("trans", None, None), P("trans", None, None),
        ),
        out_specs=(P("shock", "trans", None), spec, spec),
        check_vma=False,
    )
```

time: 392 us -> 106 us (0.27)
  the two profiles are of different devices: /device:TPU:1 before, /device:TPU:17 now
where the time goes in v1:
time: 106 us; the launch traced here: 105 us
  Pallas kernels  33.4 us (32%)
  starting transfers between devices  32.9 us (31%)
  waiting for transfers between devices  21.3 us (20%)
  other arithmetic  9.18 us (9%)
  local copies, waits for them, and re-layouts  7.39 us (7%)
    pallas_call x1, Pallas kernels, blocks(): pl.pallas_call(block_kernel, out_shape=(jax.ShapeDtypeStruct((2, 128), F3...  33.4 us
    ppermute x4, starting transfers between devices, passed_along(): return lax.ppermute(block, axis, route)  12.2 us
    ppermute x4, starting transfers between devices, extended_2(): after = lax.ppermute(first, axis, down)  11.1 us
    ppermute x4, starting transfers between devices, extended_2(): before = lax.ppermute(last, axis, up)  6.57 us
    ppermute x4, waiting for transfers between devices, extended_2(): after = lax.ppermute(first, axis, down)  6.26 us
    ppermute x2, waiting for transfers between devices, shifted(): return lax.ppermute(x, axis, [(i, (i + by) % count) for i in range(count)])  5.96 us
    ppermute x4, waiting for transfers between devices, extended_2(): before = lax.ppermute(last, axis, up)  5.03 us
    unnamed x22, local copies, waits for them, and re-layouts  4.7 us
  transfers between devices with their start and end apart: 14, of which 7 were waited for; matrix products, arithmetic and copies ran while one was open for 10% of the time, Pallas kernels for 0%

profile of v1, /device:TPU:17, one launch (start us, length us, event | category | flops | bytes accessed | tf_op | source)
XLA Modules:
  0.0 105.0 jit_solution(4271608746688913209)
XLA Ops:
  0.6 0.8 copy.35
  1.4 2.7 %collective-permute-start = (f32[2,1,3,128]{3,2,1,0:T(4,128)S(1)}, f32[2,1,3,128]{3,2,1,0:T(4,128)S(1)}, u32[]{:S(2)}, u32[]{:S(2)}) collective-permute-start(f32[2,1,3,128]{3,2,1,0:T(4,128)S(1)} %copy.35), channel_id=1, source_target_pairs={{0,1},{1,2},{2,3},{3,4},{4,5},{5,6},{6,7},{7,8},{8,9},{9,10},{10,1... | collective-permute-start | bytes 9224 | tf_op jit(solution)/shard_map/ppermute | solution.py:382
  4.1 5.3 %collective-permute-start.1 = (f32[2,1,3,128]{3,2,1,0:T(4,128)S(1)}, f32[2,1,3,128]{3,2,1,0:T(4,128)S(1)}, u32[]{:S(2)}, u32[]{:S(2)}) collective-permute-start(f32[2,1,3,128]{3,2,1,0:T(4,128)S(1)} %copy.35), channel_id=1, source_target_pairs={{1,0},{2,1},{3,2},{4,3},{5,4},{6,5},{7,6},{8,7},{9,8},{10,9},{11,1... | collective-permute-start | bytes 9224 | tf_op jit(solution)/shard_map/ppermute | solution.py:383
  9.4 5.1 %collective-permute-start.5 = (bf16[2,1,576,128]{3,2,1,0:T(8,128)(2,1)}, bf16[2,1,576,128]{3,2,1,0:T(8,128)(2,1)S(1)}, u32[]{:S(2)}, u32[]{:S(2)}) collective-permute-start(bf16[2,1,576,128]{3,2,1,0:T(8,128)(2,1)} %param.21), channel_id=1, source_target_pairs={{1,0},{2,1},{3,2},{4,3},{5,4},{6,5},{7,6},{8,7},{9,8},{10,9},{11,1... | collective-permute-start | bytes 884744 | tf_op jit(solution)/shard_map/ppermute | solution.py:383
  14.5 0.9 reduce_precision.14
  15.4 1.0 copy.46
  16.4 0.8 reduce_precision.13
  17.3 0.9 copy.43
  18.2 0.9 reduce-precision_convert_fusion
  19.8 0.8 copy.38
  21.0 0.8 pad_maximum_fusion.w_read
  23.2 0.7 pad_maximum_fusion.2.w_second
  24.1 1.0 collective-permute-done.5
  25.2 2.1 %collective-permute-start.6 = (bf16[1,3,576,128]{3,2,1,0:T(8,128)(2,1)S(1)}, bf16[1,3,576,128]{3,2,1,0:T(8,128)(2,1)S(1)}, u32[]{:S(2)}, u32[]{:S(2)}) collective-permute-start(bf16[1,3,576,128]{3,2,1,0:T(8,128)(2,1)S(1)} %get-tuple-element.63), channel_id=1, source_target_pairs={{0,16},{16,32},{32,48},{48,64},{64,80},{80,96},{96,112},{112,128},... | collective-permute-start | bytes 1327112 | tf_op jit(solution)/shard_map/ppermute | solution.py:382
  27.3 1.7 %collective-permute-start.2 = (f32[1,3,3,128]{3,2,1,0:T(4,128)S(1)}, f32[1,3,3,128]{3,2,1,0:T(4,128)S(1)}, u32[]{:S(2)}, u32[]{:S(2)}) collective-permute-start(f32[1,3,3,128]{3,2,1,0:T(4,128)S(1)} %get-tuple-element.71), channel_id=1, source_target_pairs={{0,16},{16,32},{32,48},{48,64},{64,80},{80,96},{96,112},{112,128},... | collective-permute-start | bytes 13832 | tf_op jit(solution)/shard_map/ppermute | solution.py:382
  29.0 0.7 collective-permute-start.3
  29.7 5.0 %collective-permute-done.2 = f32[1,3,3,128]{3,2,1,0:T(4,128)S(1)} collective-permute-done((f32[1,3,3,128]{3,2,1,0:T(4,128)S(1)}, f32[1,3,3,128]{3,2,1,0:T(4,128)S(1)}, u32[]{:S(2)}, u32[]{:S(2)}) %collective-permute-start.2) | collective-permute-done | bytes 4640 | tf_op jit(solution)/shard_map/ppermute | solution.py:382
  34.8 5.2 %collective-permute-done.3 = f32[1,3,3,128]{3,2,1,0:T(4,128)S(1)} collective-permute-done((f32[1,3,3,128]{3,2,1,0:T(4,128)S(1)}, f32[1,3,3,128]{3,2,1,0:T(4,128)S(1)}, u32[]{:S(2)}, u32[]{:S(2)}) %collective-permute-start.3) | collective-permute-done | bytes 4640 | tf_op jit(solution)/shard_map/ppermute | solution.py:383
  40.7 1.5 %maximum_select_fusion.feat = bf16[4,3,576,128]{3,2,1,0:T(8,128)(2,1)} fusion(bf16[1,3,576,128]{3,2,1,0:T(8,128)(2,1)S(1)} %collective-permute-done.7, bf16[2,3,576,128]{3,2,1,0:T(8,128)(2,1)S(1)} %constant_dynamic-update-slice_fusion.3, bf16[1,3,576,128]{3,2,1,0:T(8,128)(2,1)S(1)} %collective-permute-done.6, pred[4]{0:T(512)(128)(4,1)S(1)} %and_or_fusion), kind=kLoop, calls=%fused_computation | loop fusion | flops 2654208 | bytes 3538948 | tf_op jit(solution)/shard_map/jit(_where)/select_n | solution.py:413
  42.2 0.7 broadcast_in_dim.47.w_out
  42.9 33.4 %blocks.1 = (f32[2,128]{1,0:T(2,128)}, f32[4,3,3,128]{3,2,1,0:T(4,128)}) custom-call(f32[4,3,3,128]{3,2,1,0:T(4,128)} %maximum_select_fusion.1.pos, bf16[4,3,576,128]{3,2,1,0:T(8,128)(2,1)} %maximum_select_fusion.feat, s32[2,1,24,128]{3,2,1,0:T(8,128)} %codes.1, s32[2,128]{1,0:T(2,128)} %bitcast.35, bf16[64,32]{1,0:T(8,128)(2,1)} %maximum_maximum_fusion.w_first, ...), custom_call_target="tpu_custom_call" | custom-call | tf_op jit(solution)/shard_map/blocks/pallas_call | solution.py:347
  76.3 0.7 slice_bitcast_fusion
  77.7 2.8 %collective-permute-start.8 = (f32[4,3,128]{2,1,0:T(4,128)S(1)}, f32[4,3,128]{2,1,0:T(4,128)S(1)}, u32[]{:S(2)}, u32[]{:S(2)}) collective-permute-start(f32[4,3,128]{2,1,0:T(4,128)S(1)} %slice_bitcast_fusion), channel_id=1, source_target_pairs={{0,15},{1,0},{2,1},{3,2},{4,3},{5,4},{6,5},{7,6},{8,7},{9,8},{10,9... | collective-permute-start | bytes 18440 | tf_op jit(solution)/shard_map/ppermute | solution.py:390
  80.7 1.0 collective-permute-done.8
  81.7 4.9 %collective-permute-done.9 = f32[4,3,128]{2,1,0:T(4,128)S(1)} collective-permute-done((f32[4,3,128]{2,1,0:T(4,128)S(1)}, f32[4,3,128]{2,1,0:T(4,128)S(1)}, u32[]{:S(2)}, u32[]{:S(2)}) %collective-permute-start.9) | collective-permute-done | bytes 6176 | tf_op jit(solution)/shard_map/ppermute | solution.py:390
  86.6 0.7 fusion.1
  87.3 3.7 %collective-permute-start.10 = (f32[1,3,128]{2,1,0:T(4,128)S(1)}, f32[1,3,128]{2,1,0:T(4,128)S(1)}, u32[]{:S(2)}, u32[]{:S(2)}) collective-permute-start(f32[1,3,128]{2,1,0:T(4,128)S(1)} %slice_bitcast_fusion.5), channel_id=1, source_target_pairs={{16,0},{32,16},{48,32},{64,48},{80,64},{96,80},{112,96},{128,112},... | collective-permute-start | bytes 4616 | tf_op jit(solution)/shard_map/ppermute | solution.py:396
  91.1 1.9 %collective-permute-start.11 = (f32[1,3,128]{2,1,0:T(4,128)S(1)}, f32[1,3,128]{2,1,0:T(4,128)S(1)}, u32[]{:S(2)}, u32[]{:S(2)}) collective-permute-start(f32[1,3,128]{2,1,0:T(4,128)S(1)} %slice_bitcast_fusion.4), channel_id=1, source_target_pairs={{0,16},{16,32},{32,48},{48,64},{64,80},{80,96},{96,112},{112,128},... | collective-permute-start | bytes 4616 | tf_op jit(solution)/shard_map/ppermute | solution.py:396
  93.0 1.1 %collective-permute-done.11 = f32[1,3,128]{2,1,0:T(4,128)S(1)} collective-permute-done((f32[1,3,128]{2,1,0:T(4,128)S(1)}, f32[1,3,128]{2,1,0:T(4,128)S(1)}, u32[]{:S(2)}, u32[]{:S(2)}) %collective-permute-start.11) | collective-permute-done | bytes 1568 | tf_op jit(solution)/shard_map/ppermute | solution.py:396
  94.2 4.7 %collective-permute-start.12 = (f32[1,3,128]{2,1,0:T(4,128)S(1)}, f32[1,3,128]{2,1,0:T(4,128)S(1)}, u32[]{:S(2)}, u32[]{:S(2)}) collective-permute-start(f32[1,3,128]{2,1,0:T(4,128)S(1)} %get-tuple-element.76), channel_id=1, source_target_pairs={{16,0},{32,16},{48,32},{64,48},{80,64},{96,80},{112,96},{128,112},... | collective-permute-start | bytes 4616 | tf_op jit(solution)/shard_map/ppermute | solution.py:396
  98.9 1.9 %collective-permute-start.13 = (f32[1,3,128]{2,1,0:T(4,128)S(1)}, f32[1,3,128]{2,1,0:T(4,128)S(1)}, u32[]{:S(2)}, u32[]{:S(2)}) collective-permute-start(f32[1,3,128]{2,1,0:T(4,128)S(1)} %get-tuple-element.74), channel_id=1, source_target_pairs={{16,0},{32,16},{48,32},{64,48},{80,64},{96,80},{112,96},{128,112},... | collective-permute-start | bytes 4616 | tf_op jit(solution)/shard_map/ppermute | solution.py:396
  100.8 3.0 %collective-permute-done.13 = f32[1,3,128]{2,1,0:T(4,128)S(1)} collective-permute-done((f32[1,3,128]{2,1,0:T(4,128)S(1)}, f32[1,3,128]{2,1,0:T(4,128)S(1)}, u32[]{:S(2)}, u32[]{:S(2)}) %collective-permute-start.13) | collective-permute-done | bytes 1568 | tf_op jit(solution)/shard_map/ppermute | solution.py:396
  (58 shorter events, 5.5 us)
Async XLA Ops:
  0.6 23.3 %copy-start.1 = (f32[2,1,3,128]{3,1,2,0:T(1,128)S(1)}, f32[2,1,3,128]{3,1,2,0:T(1,128)}, u32[]{:S(2)}) copy-start(f32[2,1,3,128]{3,1,2,0:T(1,128)} %param.19) | copy-start | bytes 9220
  1.4 22.6 %copy-start = (bf16[2,1,576,128]{3,2,1,0:T(8,128)(2,1)S(1)}, bf16[2,1,576,128]{3,2,1,0:T(8,128)(2,1)}, u32[]{:S(2)}) copy-start(bf16[2,1,576,128]{3,2,1,0:T(8,128)(2,1)} %param.21) | copy-start | bytes 884740
  1.4 22.5 %collective-permute-start = (f32[2,1,3,128]{3,2,1,0:T(4,128)S(1)}, f32[2,1,3,128]{3,2,1,0:T(4,128)S(1)}, u32[]{:S(2)}, u32[]{:S(2)}) collective-permute-start(f32[2,1,3,128]{3,2,1,0:T(4,128)S(1)} %copy.35), channel_id=1, source_target_pairs={{0,1},{1,2},{2,3},{3,4},{4,5},{5,6},{6,7},{7,8},{8,9},{9,10},{10,1... | collective-permute-start | bytes 9224 | tf_op jit(solution)/shard_map/ppermute | solution.py:382
  4.1 19.8 %collective-permute-start.1 = (f32[2,1,3,128]{3,2,1,0:T(4,128)S(1)}, f32[2,1,3,128]{3,2,1,0:T(4,128)S(1)}, u32[]{:S(2)}, u32[]{:S(2)}) collective-permute-start(f32[2,1,3,128]{3,2,1,0:T(4,128)S(1)} %copy.35), channel_id=1, source_target_pairs={{1,0},{2,1},{3,2},{4,3},{5,4},{6,5},{7,6},{8,7},{9,8},{10,9},{11,1... | collective-permute-start | bytes 9224 | tf_op jit(solution)/shard_map/ppermute | solution.py:383
  9.4 14.5 %collective-permute-start.4 = (bf16[2,1,576,128]{3,2,1,0:T(8,128)(2,1)}, bf16[2,1,576,128]{3,2,1,0:T(8,128)(2,1)S(1)}, u32[]{:S(2)}, u32[]{:S(2)}) collective-permute-start(bf16[2,1,576,128]{3,2,1,0:T(8,128)(2,1)} %param.21), channel_id=1, source_target_pairs={{0,1},{1,2},{2,3},{3,4},{4,5},{5,6},{6,7},{7,8},{8,9},{9,10},{10,1... | collective-permute-start | bytes 884744 | tf_op jit(solution)/shard_map/ppermute | solution.py:382
  9.4 15.6 %collective-permute-start.5 = (bf16[2,1,576,128]{3,2,1,0:T(8,128)(2,1)}, bf16[2,1,576,128]{3,2,1,0:T(8,128)(2,1)S(1)}, u32[]{:S(2)}, u32[]{:S(2)}) collective-permute-start(bf16[2,1,576,128]{3,2,1,0:T(8,128)(2,1)} %param.21), channel_id=1, source_target_pairs={{1,0},{2,1},{3,2},{4,3},{5,4},{6,5},{7,6},{8,7},{9,8},{10,9},{11,1... | collective-permute-start | bytes 884744 | tf_op jit(solution)/shard_map/ppermute | solution.py:383
  25.2 15.5 %collective-permute-start.6 = (bf16[1,3,576,128]{3,2,1,0:T(8,128)(2,1)S(1)}, bf16[1,3,576,128]{3,2,1,0:T(8,128)(2,1)S(1)}, u32[]{:S(2)}, u32[]{:S(2)}) collective-permute-start(bf16[1,3,576,128]{3,2,1,0:T(8,128)(2,1)S(1)} %get-tuple-element.63), channel_id=1, source_target_pairs={{0,16},{16,32},{32,48},{48,64},{64,80},{80,96},{96,112},{112,128},... | collective-permute-start | bytes 1327112 | tf_op jit(solution)/shard_map/ppermute | solution.py:382
  27.3 13.4 %collective-permute-start.7 = (bf16[1,3,576,128]{3,2,1,0:T(8,128)(2,1)S(1)}, bf16[1,3,576,128]{3,2,1,0:T(8,128)(2,1)S(1)}, u32[]{:S(2)}, u32[]{:S(2)}) collective-permute-start(bf16[1,3,576,128]{3,2,1,0:T(8,128)(2,1)S(1)} %get-tuple-element.64), channel_id=1, source_target_pairs={{16,0},{32,16},{48,32},{64,48},{80,64},{96,80},{112,96},{128,112},... | collective-permute-start | bytes 1327112 | tf_op jit(solution)/shard_map/ppermute | solution.py:383
  27.3 7.5 %collective-permute-start.2 = (f32[1,3,3,128]{3,2,1,0:T(4,128)S(1)}, f32[1,3,3,128]{3,2,1,0:T(4,128)S(1)}, u32[]{:S(2)}, u32[]{:S(2)}) collective-permute-start(f32[1,3,3,128]{3,2,1,0:T(4,128)S(1)} %get-tuple-element.71), channel_id=1, source_target_pairs={{0,16},{16,32},{32,48},{48,64},{64,80},{80,96},{96,112},{112,128},... | collective-permute-start | bytes 13832 | tf_op jit(solution)/shard_map/ppermute | solution.py:382
  29.0 11.0 %collective-permute-start.3 = (f32[1,3,3,128]{3,2,1,0:T(4,128)S(1)}, f32[1,3,3,128]{3,2,1,0:T(4,128)S(1)}, u32[]{:S(2)}, u32[]{:S(2)}) collective-permute-start(f32[1,3,3,128]{3,2,1,0:T(4,128)S(1)} %get-tuple-element.72), channel_id=1, source_target_pairs={{16,0},{32,16},{48,32},{64,48},{80,64},{96,80},{112,96},{128,112},... | collective-permute-start | bytes 13832 | tf_op jit(solution)/shard_map/ppermute | solution.py:383
  40.7 1.5 %copy-start.5 = (f32[128]{0:T(128)S(1)}, f32[128]{0:T(128)}, u32[]{:S(2)}) copy-start(f32[128]{0:T(128)} %param.27) | copy-start | bytes 1540
  42.2 52.0 %copy-start.2 = (f32[2,1,3,128]{3,1,2,0:T(1,128)S(1)}, f32[2,1,3,128]{3,1,2,0:T(1,128)}, u32[]{:S(2)}) copy-start(f32[2,1,3,128]{3,1,2,0:T(1,128)} %param.20) | copy-start | bytes 9220
  42.2 61.6 %copy-start.3 = (f32[1,3,128]{2,0,1:T(1,128)S(1)}, f32[1,3,128]{2,0,1:T(1,128)}, u32[]{:S(2)}) copy-start(f32[1,3,128]{2,0,1:T(1,128)} %param.29) | copy-start | bytes 4612
  42.2 61.6 %copy-start.4 = (f32[1,3,128]{2,0,1:T(1,128)S(1)}, f32[1,3,128]{2,0,1:T(1,128)}, u32[]{:S(2)}) copy-start(f32[1,3,128]{2,0,1:T(1,128)} %param.28) | copy-start | bytes 4612
  77.7 4.0 %collective-permute-start.8 = (f32[4,3,128]{2,1,0:T(4,128)S(1)}, f32[4,3,128]{2,1,0:T(4,128)S(1)}, u32[]{:S(2)}, u32[]{:S(2)}) collective-permute-start(f32[4,3,128]{2,1,0:T(4,128)S(1)} %slice_bitcast_fusion), channel_id=1, source_target_pairs={{0,15},{1,0},{2,1},{3,2},{4,3},{5,4},{6,5},{7,6},{8,7},{9,8},{10,9... | collective-permute-start | bytes 18440 | tf_op jit(solution)/shard_map/ppermute | solution.py:390
  80.5 6.1 %collective-permute-start.9 = (f32[4,3,128]{2,1,0:T(4,128)S(1)}, f32[4,3,128]{2,1,0:T(4,128)S(1)}, u32[]{:S(2)}, u32[]{:S(2)}) collective-permute-start(f32[4,3,128]{2,1,0:T(4,128)S(1)} %slice_bitcast_fusion.1), channel_id=1, source_target_pairs={{0,1},{1,2},{2,3},{3,4},{4,5},{5,6},{6,7},{7,8},{8,9},{9,10},{10,1... | collective-permute-start | bytes 18440 | tf_op jit(solution)/shard_map/ppermute | solution.py:390
  87.3 5.7 %collective-permute-start.10 = (f32[1,3,128]{2,1,0:T(4,128)S(1)}, f32[1,3,128]{2,1,0:T(4,128)S(1)}, u32[]{:S(2)}, u32[]{:S(2)}) collective-permute-start(f32[1,3,128]{2,1,0:T(4,128)S(1)} %slice_bitcast_fusion.5), channel_id=1, source_target_pairs={{16,0},{32,16},{48,32},{64,48},{80,64},{96,80},{112,96},{128,112},... | collective-permute-start | bytes 4616 | tf_op jit(solution)/shard_map/ppermute | solution.py:396
  91.1 3.1 %collective-permute-start.11 = (f32[1,3,128]{2,1,0:T(4,128)S(1)}, f32[1,3,128]{2,1,0:T(4,128)S(1)}, u32[]{:S(2)}, u32[]{:S(2)}) collective-permute-start(f32[1,3,128]{2,1,0:T(4,128)S(1)} %slice_bitcast_fusion.4), channel_id=1, source_target_pairs={{0,16},{16,32},{32,48},{48,64},{64,80},{80,96},{96,112},{112,128},... | collective-permute-start | bytes 4616 | tf_op jit(solution)/shard_map/ppermute | solution.py:396
  94.2 6.6 %collective-permute-start.12 = (f32[1,3,128]{2,1,0:T(4,128)S(1)}, f32[1,3,128]{2,1,0:T(4,128)S(1)}, u32[]{:S(2)}, u32[]{:S(2)}) collective-permute-start(f32[1,3,128]{2,1,0:T(4,128)S(1)} %get-tuple-element.76), channel_id=1, source_target_pairs={{16,0},{32,16},{48,32},{64,48},{80,64},{96,80},{112,96},{128,112},... | collective-permute-start | bytes 4616 | tf_op jit(solution)/shard_map/ppermute | solution.py:396
  98.9 4.9 %collective-permute-start.13 = (f32[1,3,128]{2,1,0:T(4,128)S(1)}, f32[1,3,128]{2,1,0:T(4,128)S(1)}, u32[]{:S(2)}, u32[]{:S(2)}) collective-permute-start(f32[1,3,128]{2,1,0:T(4,128)S(1)} %get-tuple-element.74), channel_id=1, source_target_pairs={{16,0},{32,16},{48,32},{64,48},{80,64},{96,80},{112,96},{128,112},... | collective-permute-start | bytes 4616 | tf_op jit(solution)/shard_map/ppermute | solution.py:396

commit v2 on v1

--- a/solution.py
+++ b/solution.py
@@ -5,6 +5,7 @@
 from jax import lax
 from jax.experimental import pallas as pl
 from jax.experimental.pallas import tpu as pltpu
+from jax.sharding import PartitionSpec as P
 
 CUTOFF_RADIUS = 9.5
 BLOCK_LENGTH = 13.2
@@ -66,7 +67,7 @@
         x2 = x * x
         x4 = x2 * x2
         slot = lax.broadcasted_iota(jnp.int32, (8, 128), 0) + 8 * part
-        live = jnp.where(slot < counts[pl.ds(r, 8, stride=0), :], 1.0 / 24.0, 0.0)
+        live = jnp.where(slot < counts[r, pl.ds(0, 8, stride=0), :], 1.0 / 24.0, 0.0)
         env = (1.0 + x4 * x2 * (-28.0 + x * (48.0 - 21.0 * x))) * live
         slope = (-168.0 / CUTOFF_RADIUS) * x4 * x * ((1.0 - x) * (1.0 - x)) * live
         r3, r5, r15 = math.sqrt(3.0), math.sqrt(5.0), math.sqrt(15.0)
@@ -199,11 +200,16 @@
     sig = sigmoid(z)
     act = z * sig
     energy = jnp.sum(w_out * act, axis=0, keepdims=True)
-    energies[0:1, :] = energy[:, :128]
-    energies[1:2, :] = energy[:, 128:]
+    energies[0] = energy[:, :128]
+    energies[1] = energy[:, 128:]
     gz = w_out * (sig + act * (1.0 - sig))
     hi, lo = split(gz)
-    gs = jnp.dot(read_t3, jnp.concatenate([hi, lo, hi], axis=0), preferred_element_type=F32)
+    gs = lax.dot_general(
+        read_t3,
+        jnp.concatenate([hi, lo, hi], axis=0),
+        (((0,), (0,)), ((), ())),
+        preferred_element_type=F32,
+    )
     gs = gs + gs
     for r in range(2):
         g = gs[:, 128 * r : 128 * r + 128]
@@ -278,38 +284,166 @@
     lax.fori_loop(0, 24, body, 0, unroll=2)
     out = lax.dot_general(lhs[...], hot[...], (((1,), (1,)), ((), ())), preferred_element_type=F32)
     for b in range(9):
-        at = (r + b // 3, b % 3)
         for q in range(3):
             v = -(out[8 * b + q : 8 * b + q + 1] + out[8 * b + q + 3 : 8 * b + q + 4])
             if b == 4:
                 v += centre[q]
-            forces[at[0], at[1], q : q + 1, :] += v
-
-
-def split_whole(w):
-    rounded = lax.reduce_precision(w, 8, 7)
-    return rounded.astype(BF16), (w - rounded).astype(BF16)
-
-
-def stack3(w):
-    hi, lo = split_whole(w)
-    return jnp.concatenate([hi, hi, lo], axis=1)
-
-
-def block_kernel(
-    pos, feat, codes, counts, w_first, w_second, w_read, w_read_t, w_out, energies, forces,
-    geo, unit, basis, hid, wgt, window, got, agg, slopes, edge, lhs, hot,
+            forces[b % 3, r + b // 3, q : q + 1, :] += v
+
+
+def stack(w, axis):
+    hi, lo = split(w)
+    return jnp.concatenate([hi, hi, lo], axis=axis)
+
+
+POS = 0
+VEL = 8
+OWN = 9
+CHIP = 11
+OFF = 12
+CORNER = 13
+FAR = 14
+NEAR_CHIP = 16
+FAR_CHIP = 17
+FAR_CORNER = 18
+TAIL = 19
+COPIES = 24
+AROUND = ((-1, -1), (-1, 0), (-1, 1), (0, -1), (0, 1), (1, -1), (1, 0), (1, 1))
+BACK = ((0, 1), (0, -1), (-1, 1), (-1, 0), (-1, -1))
+
+
+def step_kernel(
+    positions, velocities, features, codes, counts, w_first, w_second, w_read, w_out,
+    fresh_pos, fresh_vel, energies, new_pos, new_vel,
+    pos, vel_in, fx, geo, unit, basis, hid, wgt, window, got, agg, slopes, edge, lhs, hot,
+    forces, tail, first, second, read3, read_t3, out_col, own_sem, send_sem, recv_sem,
 ):
+    s = lax.axis_index("shock")
+    t = lax.axis_index("trans")
+    ns = lax.axis_size("shock")
+    nt = lax.axis_size("trans")
+    core = lax.rem(s, 2)
+    way = 1 - 2 * lax.rem(t, 2)
+    out_way = 2 * core - 1
+
+    def at(ds, dt):
+        return (lax.rem(s + ds + ns, ns), lax.rem(t + dt + nt, nt))
+
+    def copy(k, src, dst, to):
+        return pltpu.make_async_remote_copy(
+            src_ref=src,
+            dst_ref=dst,
+            send_sem=send_sem.at[k],
+            recv_sem=recv_sem.at[k],
+            device_id=to,
+            device_id_type=pl.DeviceIdType.MESH,
+        )
+
+    barrier = pltpu.get_barrier_semaphore()
+    for ds, dt in AROUND + ((0, 2), (0, -2)):
+        pl.semaphore_signal(
+            barrier, inc=1, device_id=at(ds, dt), device_id_type=pl.DeviceIdType.MESH
+        )
+    own = pltpu.make_async_copy(features.at[:, 0], fx.at[pl.ds(1, 2), 1], own_sem)
+    own.start()
+    pos[1:3, 1] = positions[:, 0]
+    pl.semaphore_wait(barrier, 10)
+
+    flights = {}
+    for i, (ds, dt) in enumerate(AROUND):
+        if ds == 0:
+            src, dst = positions.at[:, 0], pos.at[pl.ds(1, 2), 1 - dt]
+        elif ds == 1:
+            src, dst = positions.at[1, 0], pos.at[0, 1 - dt]
+        else:
+            src, dst = positions.at[0, 0], pos.at[3, 1 - dt]
+        flights[POS + i] = copy(POS + i, src, dst, at(ds, dt))
+    flights[VEL] = copy(VEL, velocities.at[0, 0], vel_in, at(-1, 0))
+    near, far = 1 + way, 1 - way
+    for i in range(2):
+        flights[OWN + i] = copy(OWN + i, features.at[i, 0], fx.at[1 + i, far], at(0, way))
+    chip_row, chip_ghost = 1 - core, 3 * core
+    off_row, off_ghost = core, 3 * (1 - core)
+    flights[CHIP] = copy(CHIP, features.at[chip_row, 0], fx.at[chip_ghost, 1], at(-out_way, 0))
+    flights[OFF] = copy(OFF, features.at[off_row, 0], fx.at[off_ghost, 1], at(out_way, 0))
+    flights[CORNER] = copy(
+        CORNER, features.at[off_row, 0], fx.at[off_ghost, far], at(out_way, way)
+    )
+    for k in list(range(POS, POS + 8)) + [OWN, OWN + 1, CORNER, OFF, CHIP, VEL]:
+        flights[k].start()
+    my_chip_ghost, my_off_ghost = 3 * (1 - core), 3 * core
+    for i in range(2):
+        flights[FAR + i] = copy(
+            FAR + i, fx.at[1 + i, near], fx.at[1 + i, far], at(0, 2 * way)
+        )
+    flights[FAR_CORNER] = copy(
+        FAR_CORNER, fx.at[my_off_ghost, near], fx.at[my_off_ghost, far], at(0, 2 * way)
+    )
+    flights[NEAR_CHIP] = copy(
+        NEAR_CHIP, fx.at[1 + chip_row, near], fx.at[chip_ghost, near], at(-out_way, 0)
+    )
+    flights[FAR_CHIP] = copy(
+        FAR_CHIP, fx.at[1 + chip_row, far], fx.at[chip_ghost, far], at(-out_way, 0)
+    )
+
+    first[...] = jnp.concatenate([stack(w_first[...], 1), jnp.zeros((64, 8), BF16)], axis=1)
+    second[...] = stack(w_second[...], 1)
+    read3[...] = stack(w_read[...], 1)
+    read_t3[...] = stack(w_read[...], 0)
+    col = jnp.broadcast_to(w_out[...], (128, 128)).T
+    out_col[...] = jnp.concatenate([col, col], axis=1)
+
+    for k in range(POS, POS + 8):
+        flights[k].wait_recv()
+
+    @pl.when(s == 0)
+    def _():
+        pos[0] = jnp.zeros((3, 3, 128), F32)
+
+    @pl.when(s == ns - 1)
+    def _():
+        pos[3] = jnp.zeros((3, 3, 128), F32)
+
     for r in range(2):
         geometry(r, pos, codes, counts, geo, unit)
+
+    def radial_steps(lo, hi):
+        def radial_step(step, carry):
+            radial(step, geo, first[...], second[...], basis, hid, wgt)
+            return carry
+
+        lax.fori_loop(lo, hi, radial_step, 0)
+
+    total = 48 // SPAN
+    radial_steps(0, total // 4)
+    for i in range(2):
+        flights[OWN + i].wait_recv()
+        flights[FAR + i].start()
+    flights[NEAR_CHIP].start()
+    radial_steps(total // 4, total // 2)
+    flights[CORNER].wait_recv()
+    flights[FAR_CORNER].start()
+    radial_steps(total // 2, total)
+    for i in range(2):
+        flights[FAR + i].wait_recv()
+    flights[FAR_CHIP].start()
+    own.wait()
+    for k in (CHIP, OFF, NEAR_CHIP, FAR_CORNER, FAR_CHIP, VEL):
+        flights[k].wait_recv()
+    for k in range(TAIL):
+        flights[k].wait_send()
+
+    @pl.when(s == 0)
+    def _():
+        fx[0] = jnp.zeros((3, 576, 128), BF16)
+
+    @pl.when(s == ns - 1)
+    def _():
+        fx[3] = jnp.zeros((3, 576, 128), BF16)
+
+    for r in range(2):
         for b in range(9):
-            window[r, :, 128 * b : 128 * b + 128] = feat[r + b // 3, b % 3]
-
-    def radial_step(step, carry):
-        radial(step, geo, w_first[...], w_second[...], basis, hid, wgt)
-        return carry
-
-    lax.fori_loop(0, 48 // SPAN, radial_step, 0)
+            window[r, :, 128 * b : 128 * b + 128] = fx[r + b // 3, b % 3]
 
     def gather_step(step, carry):
         gather(step, codes, window, got)
@@ -322,7 +456,7 @@
         return carry
 
     lax.fori_loop(0, 2 * (64 // TILE), aggregate_step, 0)
-    readout(agg, w_read[...], w_read_t[...], w_out[...], energies)
+    readout(agg, read3[...], read_t3[...], out_col[...], energies)
 
     def backward_step(step, carry):
         backward(step, geo, wgt, got, agg, slopes)
@@ -334,25 +468,45 @@
         centre = edge_forces(r, geo, unit, slopes, edge)
         scatter(r, codes, edge, lhs, hot, centre, forces)
 
-
-def weights(w_first, w_second, w_read, w_out):
-    hi, lo = split_whole(w_first)
-    first = jnp.concatenate([hi, hi, lo, jnp.zeros_like(hi)], axis=1)
-    out = jnp.broadcast_to(w_out[:, None], (w_out.shape[0], 256))
-    return first, stack3(w_second), stack3(w_read), stack3(w_read.T), out
-
-
-def blocks(pos_ext, feat_ext, codes, counts, w):
+    for i, (ds, dt) in enumerate(BACK):
+        src = forces.at[1 + dt, pl.ds(2 if ds == 0 else 0, 2)]
+        flights[TAIL + i] = copy(TAIL + i, src, tail.at[i], at(ds, dt))
+        flights[TAIL + i].start()
+    for i in range(5):
+        flights[TAIL + i].wait_recv()
+    front = s == ns - 1
+    above = tail[2] + tail[3] + tail[4]
+    force = forces[1, 2:4] + tail[0] + tail[1] + jnp.where(front, 0.0, above)
+    force = force[:, 0:3]
+    vel = velocities[1, 0] + KICK_FACTOR * force[0]
+    new_vel[0, 0] = vel
+    new_pos[0, 0] = positions[1, 0] + MOVE_FACTOR * vel
+    vel = vel_in[...] + KICK_FACTOR * force[1]
+    new_vel[1, 0] = jnp.where(front, fresh_vel[0], vel)
+    new_pos[1, 0] = jnp.where(front, fresh_pos[0], pos[3, 1] + MOVE_FACTOR * vel)
+    for i in range(5):
+        flights[TAIL + i].wait_send()
+
+
+def local(
+    positions, velocities, features, neighbours, counts, w_first, w_second, w_read, w_out,
+    fresh_positions, fresh_velocities,
+):
     vmem = pl.BlockSpec(memory_space=pltpu.VMEM)
+    whole = pl.BlockSpec(memory_space=pl.ANY)
     return pl.pallas_call(
-        block_kernel,
+        step_kernel,
         out_shape=(
-            jax.ShapeDtypeStruct((2, 128), F32),
-            jax.ShapeDtypeStruct((4, 3, 3, 128), F32),
+            jax.ShapeDtypeStruct((2, 1, 128), F32),
+            jax.ShapeDtypeStruct((2, 1, 3, 128), F32),
+            jax.ShapeDtypeStruct((2, 1, 3, 128), F32),
         ),
-        in_specs=[vmem] * 9,
-        out_specs=(vmem, vmem),
+        in_specs=[vmem, vmem, whole] + [vmem] * 8,
+        out_specs=(vmem, vmem, vmem),
         scratch_shapes=[
+            pltpu.VMEM((4, 3, 3, 128), F32),
+            pltpu.VMEM((3, 128), F32),
+            pltpu.VMEM((4, 3, 576, 128), BF16),
             pltpu.VMEM((2, GEO, 24, 128), F32),
             pltpu.VMEM((2, 3, 24, 128), F32),
             pltpu.VMEM((32, 256 * SPAN), BF16),
@@ -365,74 +519,25 @@
             pltpu.VMEM((3, 24, 128), F32),
             pltpu.VMEM((80, 3072), BF16),
             pltpu.VMEM((128, 3072), BF16),
+            pltpu.VMEM((3, 4, 8, 128), F32),
+            pltpu.VMEM((5, 2, 8, 128), F32),
+            pltpu.VMEM((64, 32), BF16),
+            pltpu.VMEM((192, 192), BF16),
+            pltpu.VMEM((128, 576), BF16),
+            pltpu.VMEM((384, 192), BF16),
+            pltpu.VMEM((128, 256), F32),
+            pltpu.SemaphoreType.DMA,
+            pltpu.SemaphoreType.DMA((COPIES,)),
+            pltpu.SemaphoreType.DMA((COPIES,)),
         ],
-        compiler_params=pltpu.CompilerParams(vmem_limit_bytes=56 << 20),
-        name="blocks",
-    )(pos_ext, feat_ext, codes, counts, *w)
-from jax.sharding import PartitionSpec as P
-
-
-def extended_2(x, sides, width):
-    for axis, dim in sides:
-        count, length = (lax.axis_size(axis), x.shape[dim])
-        up = [(i, (i + 1) % count) for i in range(count)]
-        down = [(j, i) for i, j in up]
-        last = lax.slice_in_dim(x, length - width, length, axis=dim)
-        first = lax.slice_in_dim(x, 0, width, axis=dim)
-        before = lax.ppermute(last, axis, up)
-        after = lax.ppermute(first, axis, down)
-        x = jnp.concatenate([before, x, after], axis=dim)
-    return x
-
-
-def shifted(x, axis, by):
-    count = lax.axis_size(axis)
-    return lax.ppermute(x, axis, [(i, (i + by) % count) for i in range(count)])
-
-
-def passed_along(block, axis, distance):
-    devices = range(lax.axis_size(axis))
-    route = [(i - distance, i) for i in devices if i - distance in devices]
-    return lax.ppermute(block, axis, route)
-
-
-def local(
-    positions, velocities, features, neighbours, counts, w_first, w_second, w_read, w_out,
-    fresh_positions, fresh_velocities,
-):
-    nrows, ncols = (positions.shape[0], positions.shape[1])
-    shock_place = lax.axis_index("shock")
-    front = lax.axis_size("shock") - 1
-    pos_ext = extended_2(positions, (("trans", 1), ("shock", 0)), 1)
-    feat_ext = extended_2(features, (("trans", 1), ("shock", 0)), 1)
-    ext_rows = lax.broadcasted_iota(jnp.int32, (nrows + 2, 1, 1, 1), 0)
-    outside = (ext_rows == 0) & (shock_place == 0) | (ext_rows == nrows + 1) & (
-        shock_place == front
-    )
-    pos_ext = jnp.where(outside, jnp.zeros((), jnp.float32), pos_ext)
-    feat_ext = jnp.where(outside, jnp.zeros((), jnp.bfloat16), feat_ext)
-    energies, forces_ext = blocks(
-        pos_ext, feat_ext, neighbours, counts[:, 0], weights(w_first, w_second, w_read, w_out)
-    )
-    from_right = shifted(forces_ext[:, 0], "trans", -1)
-    from_left = shifted(forces_ext[:, ncols + 1], "trans", 1)
-    folded = forces_ext[:, 1 : ncols + 1]
-    folded = folded.at[:, ncols - 1].add(from_right)
-    folded = folded.at[:, 0].add(from_left)
-    partial_force = folded[1 : nrows + 1]
-    from_front = passed_along(folded[0], "shock", -1)
-    from_rear = passed_along(folded[nrows + 1], "shock", 1)
-    total_force = partial_force.at[nrows - 1].add(from_front)
-    total_force = total_force.at[0].add(from_rear)
-    new_vel = velocities + KICK_FACTOR * total_force
-    moved = positions + MOVE_FACTOR * new_vel
-    incoming_pos, incoming_vel = passed_along((moved[0], new_vel[0]), "shock", -1)
-    at_front = shock_place == front
-    last_pos = jnp.where(at_front, fresh_positions, incoming_pos)
-    last_vel = jnp.where(at_front, fresh_velocities, incoming_vel)
-    new_positions = jnp.concatenate([moved[1:], last_pos[None]], axis=0)
-    new_velocities = jnp.concatenate([new_vel[1:], last_vel[None]], axis=0)
-    return (energies[:, None], new_positions, new_velocities)
+        compiler_params=pltpu.CompilerParams(
+            vmem_limit_bytes=56 << 20, collective_id=0, has_side_effects=True
+        ),
+        name="step",
+    )(
+        positions, velocities, features, neighbours, counts, w_first, w_second, w_read,
+        w_out[None], fresh_positions, fresh_velocities,
+    )
 
 
 def solution(mesh):

time: 106 us -> 69 us (0.65)
  the two profiles are of different devices: /device:TPU:17 before, /device:TPU:1 now
where the time goes in v2:
time: 69 us; the launch traced here: 67.6 us
  Pallas kernels  58.3 us (84%)
  local copies, waits for them, and re-layouts  8.68 us (13%)
    pallas_call x1, Pallas kernels, local(): pl.pallas_call(step_kernel, out_shape=(jax.ShapeDtypeStruct((2, 1, 128),...  58.3 us
    unnamed x26, local copies, waits for them, and re-layouts  7.52 us

profile of v2, /device:TPU:1, one launch (start us, length us, event | category | flops | bytes accessed | tf_op | source)
XLA Modules:
  0.0 67.6 jit_solution(305828167889553184)
XLA Ops:
  0.6 0.0 copy-start.6
  0.6 0.0 copy-start.7
  0.7 0.7 copy-done.6
  1.3 0.0 copy-start.4
  1.3 0.6 copy.19.fresh_pos
  1.9 0.0 copy-done.7
  1.9 0.6 copy.20.fresh_vel
  2.5 0.0 copy-done.4
  2.5 0.0 copy-start.5
  2.5 0.6 copy.14.positions
  3.1 0.1 copy-done.5
  3.2 0.0 copy-start.1
  3.2 0.6 copy.15.velocities
  3.8 0.1 copy-done.1
  3.9 0.0 copy-start
  3.9 0.7 %copy.16.w_first = f32[64,8]{1,0:T(8,128)} copy(f32[64,8]{0,1:T(8,128)S(1)} %copy-done.1) | data formatting | bytes 4096 | tf_op args[5]
  4.5 1.6 %copy.17.w_second = f32[192,64]{1,0:T(8,128)} copy(f32[192,64]{0,1:T(8,128)} %param.17) | data formatting | bytes 98304 | tf_op args[6]
  6.1 0.0 copy-done
  6.1 0.7 %copy.18.w_read = f32[128,192]{1,0:T(8,128)} copy(f32[128,192]{0,1:T(8,128)S(1)} %copy-done) | data formatting | bytes 196608 | tf_op args[7]
  6.9 58.3 %step.1 = (f32[2,1,128]{2,1,0:T(1,128)}, f32[2,1,3,128]{3,2,1,0:T(4,128)}, f32[2,1,3,128]{3,2,1,0:T(4,128)}) custom-call(f32[2,1,3,128]{3,2,1,0:T(4,128)} %copy.14.positions, f32[2,1,3,128]{3,2,1,0:T(4,128)} %copy.15.velocities, bf16[2,1,576,128]{3,2,1,0:T(8,128)(2,1)} %features.1, s32[2,1,24,128]{3,2,1,0:T(8,128)} %codes.1, s32[2,1,128]{2,1,0:T(1,128)} %counts.1, ...), custom_call_target="tpu_custom_call" | custom-call | tf_op jit(solution)/shard_map/step/pallas_call | solution.py:497
  65.2 0.0 copy-start.3
  65.2 0.0 copy-start.2
  65.2 0.7 copy-done.3
  65.8 0.6 copy.21
  66.4 0.0 copy-done.2
  66.4 0.0 copy-start.8
  66.4 0.6 copy.22
  67.0 0.1 copy-done.8
  67.1 0.6 copy.24
Async XLA Ops:
  0.6 0.7 %copy-start.6 = (f32[1,3,128]{2,0,1:T(1,128)S(1)}, f32[1,3,128]{2,0,1:T(1,128)}, u32[]{:S(2)}) copy-start(f32[1,3,128]{2,0,1:T(1,128)} %param.20) | copy-start | bytes 4612
  0.6 1.3 %copy-start.7 = (f32[1,3,128]{2,0,1:T(1,128)S(1)}, f32[1,3,128]{2,0,1:T(1,128)}, u32[]{:S(2)}) copy-start(f32[1,3,128]{2,0,1:T(1,128)} %param.21) | copy-start | bytes 4612
  1.3 1.2 %copy-start.4 = (f32[2,1,3,128]{3,1,2,0:T(1,128)S(1)}, f32[2,1,3,128]{3,1,2,0:T(1,128)}, u32[]{:S(2)}) copy-start(f32[2,1,3,128]{3,1,2,0:T(1,128)} %param.11) | copy-start | bytes 9220
  2.5 0.7 %copy-start.5 = (f32[2,1,3,128]{3,1,2,0:T(1,128)S(1)}, f32[2,1,3,128]{3,1,2,0:T(1,128)}, u32[]{:S(2)}) copy-start(f32[2,1,3,128]{3,1,2,0:T(1,128)} %param.12) | copy-start | bytes 9220
  3.2 0.7 %copy-start.1 = (f32[64,8]{0,1:T(8,128)S(1)}, f32[64,8]{0,1:T(8,128)}, u32[]{:S(2)}) copy-start(f32[64,8]{0,1:T(8,128)} %param.16) | copy-start | bytes 6148
  3.9 2.3 %copy-start = (f32[128,192]{0,1:T(8,128)S(1)}, f32[128,192]{0,1:T(8,128)}, u32[]{:S(2)}) copy-start(f32[128,192]{0,1:T(8,128)} %param.18) | copy-start | bytes 294916
  65.2 0.7 copy-start.3
  65.2 1.2 %copy-start.2 = (f32[2,1,3,128]{3,2,1,0:T(4,128)S(1)}, f32[2,1,3,128]{3,2,1,0:T(4,128)}, u32[]{:S(2)}) copy-start(f32[2,1,3,128]{3,2,1,0:T(4,128)} %get-tuple-element.5) | copy-start | bytes 9220
  66.4 0.7 copy-start.8

commit v3 on v2

--- a/solution.py
+++ b/solution.py
@@ -14,7 +14,7 @@
 F32 = jnp.float32
 BF16 = jnp.bfloat16
 GEO = 12
-SPAN = 4
+SPAN = 24
 
 
 def split(x):
@@ -39,7 +39,27 @@
     return s * sign, c * sign
 
 
-def geometry(r, pos, codes, counts, geo, unit):
+def block_at(r, kk):
+    if kk < 2:
+        return 1 + kk, 0
+    if kk == 2:
+        return 3 * r, 0
+    return r + (kk - 3) % 3, (kk - 3) // 3 + 1
+
+
+def places(r, way, codes, place):
+    code = codes[r, 0]
+    cell = code >> 7
+    iz = (cell >= 9).astype(jnp.int32) + (cell >= 18).astype(jnp.int32)
+    k = cell - 9 * iz
+    is_ = (k >= 3).astype(jnp.int32) + (k >= 6).astype(jnp.int32)
+    it = k - 3 * is_ - 1
+    centre = jnp.where(is_ == 0, 2, is_ - 1) if r == 0 else is_
+    kk = jnp.where(it == 0, centre, jnp.where(it == way, 3, 6) + is_)
+    place[r] = kk * 128 + (code & 127)
+
+
+def geometry(r, pos, codes, place, counts, geo, unit):
     for part in range(3):
         rows = slice(8 * part, 8 * part + 8)
         code = codes[r, 0, rows, :]
@@ -49,15 +69,17 @@
         k = cell - 9 * iz
         is_ = (k >= 3).astype(jnp.int32) + (k >= 6).astype(jnp.int32)
         it = k - 3 * is_
+        kk = place[r, rows, :] >> 7
         shifts = [(v - 1).astype(F32) * BLOCK_LENGTH for v in (is_, it, iz)]
         delta = []
         for comp in range(3):
             other = jnp.zeros((8, 128), F32)
             for b in range(9):
-                row = pos[r + b // 3, b % 3, pl.ds(comp, 8, stride=0), :]
+                row, role = block_at(r, b)
+                row = pos[row, role, comp, pl.ds(0, 8, stride=0), :]
                 got = jnp.take_along_axis(row, j, axis=1, mode="promise_in_bounds")
-                other = jnp.where(k == b, got, other)
-            centre = pos[r + 1, 1, pl.ds(comp, 8, stride=0), :]
+                other = jnp.where(kk == b, got, other)
+            centre = pos[r + 1, 0, comp, pl.ds(0, 8, stride=0), :]
             delta.append(other + shifts[comp] - centre)
         dx, dy, dz = delta
         d = jnp.sqrt(dx * dx + dy * dy + dz * dz)
@@ -132,26 +154,39 @@
         wgt[r, n0 + q, 1] = w[:, 128 * (SPAN + q) : 128 * (SPAN + q) + 128]
 
 
-def gather(step, codes, window, got):
-    r = step // 12
-    n0 = (step % 12) * 2
+STAGES = ((0, 2), (2, 6), (6, 9))
+
+
+def gather(r, stage, step, place, fx, got):
+    n0 = step * 2
+    first, last = STAGES[stage]
     ids = lax.broadcasted_iota(jnp.int32, (128, 128), 0).astype(F32).astype(BF16)
     halves = []
     for q in range(2):
-        code = codes[r, 0, pl.ds(n0 + q, 16, stride=0), :]
-        j = (code & 127).astype(F32)
-        cell = code >> 7
-        k = cell - 9 * ((cell >= 9).astype(jnp.int32) + (cell >= 18).astype(jnp.int32))
+        at = place[r, pl.ds(n0 + q, 16, stride=0), :]
+        j = (at & 127).astype(F32)
+        kk = at >> 7
         pieces = []
-        for b in range(9):
-            val = jnp.where(k == b, j, -1.0).astype(BF16)
+        for b in range(first, last):
+            val = jnp.where(kk == b, j, -1.0).astype(BF16)
             val = jnp.concatenate([val] * 8, axis=0)
             pieces.append(jnp.where(val == ids, jnp.ones((), BF16), jnp.zeros((), BF16)))
         halves.append(jnp.concatenate(pieces, axis=0))
     hot = jnp.concatenate(halves, axis=1)
-    out = jnp.dot(window[r], hot, preferred_element_type=F32)
-    got[r, n0] = out[:, :128]
-    got[r, n0 + 1] = out[:, 128:]
+    rows = [fx[block_at(r, b)] for b in range(first, last)]
+    out = jnp.dot(jnp.concatenate(rows, axis=1), hot, preferred_element_type=F32)
+    for q in range(2):
+        part = out[:, 128 * q : 128 * q + 128]
+        got[r, n0 + q] = part if stage == 0 else got[r, n0 + q] + part
+
+
+def hot_rows(r, place, hot_t):
+    j = (place[r] & 127).astype(F32)
+    cols = jnp.concatenate([j, jnp.zeros((104, 128), F32)], axis=0).T
+    ids = lax.broadcasted_iota(jnp.int32, (128, 128), 1).astype(F32)
+    for n in range(24):
+        same = jnp.broadcast_to(cols[:, n : n + 1], (128, 128)) == ids
+        hot_t[r, 128 * n : 128 * n + 128, :] = jnp.where(same, 1.0, 0.0).astype(BF16)
 
 
 def row8(ref, r, q, n, times=1):
@@ -179,7 +214,7 @@
             acc[m] += p0 * y[m] + w[1] * x[m]
         return tuple(acc)
 
-    acc = lax.fori_loop(0, 24, body, (jnp.zeros((TILE, 128), F32),) * 9, unroll=4)
+    acc = lax.fori_loop(0, 24, body, (jnp.zeros((TILE, 128), F32),) * 9, unroll=8)
     for m in range(9):
         agg[r, m, pl.ds(c0, TILE), :] = acc[m]
 
@@ -204,12 +239,7 @@
     energies[1] = energy[:, 128:]
     gz = w_out * (sig + act * (1.0 - sig))
     hi, lo = split(gz)
-    gs = lax.dot_general(
-        read_t3,
-        jnp.concatenate([hi, lo, hi], axis=0),
-        (((0,), (0,)), ((), ())),
-        preferred_element_type=F32,
-    )
+    gs = jnp.dot(read_t3, jnp.concatenate([hi, lo, hi], axis=0), preferred_element_type=F32)
     gs = gs + gs
     for r in range(2):
         g = gs[:, 128 * r : 128 * r + 128]
@@ -260,35 +290,30 @@
     return out
 
 
-def scatter(r, codes, edge, lhs, hot, centre, forces):
-    ids = lax.broadcasted_iota(jnp.int32, (128, 128), 0).astype(F32).astype(BF16)
+def scatter(r, place, edge, lhs, hot_t, centre, forces):
     pick = lax.broadcasted_iota(jnp.int32, (8, 128), 0)
 
     def body(n, carry):
-        code = codes[r, 0, pl.ds(n, 8, stride=0), :]
-        cell = code >> 7
-        k = cell - 9 * ((cell >= 9).astype(jnp.int32) + (cell >= 18).astype(jnp.int32))
+        kk = place[r, pl.ds(n, 8, stride=0), :] >> 7
         value = jnp.zeros((8, 128), F32)
         for q in range(3):
             f = edge[q, pl.ds(n, 8, stride=0), :]
             hi = f.astype(BF16).astype(F32)
             value = jnp.where(pick == q, hi, jnp.where(pick == q + 3, f - hi, value))
-        rows = [jnp.where(k == b, value, 0.0) for b in range(9)] + [jnp.zeros((8, 128), F32)]
+        rows = [jnp.where(kk == b, value, 0.0) for b in range(9)] + [jnp.zeros((8, 128), F32)]
         lanes = pl.ds(pl.multiple_of(n * 128, 128), 128)
         lhs[:, lanes] = jnp.concatenate(rows, axis=0).astype(BF16)
-        j = (codes[r, 0, pl.ds(n, 16, stride=0), :] & 127).astype(F32).astype(BF16)
-        j = jnp.concatenate([j] * 8, axis=0)
-        hot[:, lanes] = jnp.where(j == ids, jnp.ones((), BF16), jnp.zeros((), BF16))
         return carry
 
-    lax.fori_loop(0, 24, body, 0, unroll=2)
-    out = lax.dot_general(lhs[...], hot[...], (((1,), (1,)), ((), ())), preferred_element_type=F32)
+    lax.fori_loop(0, 24, body, 0, unroll=4)
+    out = jnp.dot(lhs[...], hot_t[r], preferred_element_type=F32)
     for b in range(9):
+        row, role = block_at(r, b)
         for q in range(3):
             v = -(out[8 * b + q : 8 * b + q + 1] + out[8 * b + q + 3 : 8 * b + q + 4])
-            if b == 4:
+            if row == r + 1 and role == 0:
                 v += centre[q]
-            forces[b % 3, r + b // 3, q : q + 1, :] += v
+            forces[role, row, q] += v
 
 
 def stack(w, axis):
@@ -313,10 +338,11 @@
 
 
 def step_kernel(
-    positions, velocities, features, codes, counts, w_first, w_second, w_read, w_out,
-    fresh_pos, fresh_vel, energies, new_pos, new_vel,
-    pos, vel_in, fx, geo, unit, basis, hid, wgt, window, got, agg, slopes, edge, lhs, hot,
-    forces, tail, first, second, read3, read_t3, out_col, own_sem, send_sem, recv_sem,
+    positions_in, velocities_in, features, codes_in, counts_in, w_first_in, w_second_in, w_read_in,
+    w_out_in, fresh_pos_in, fresh_vel_in, energies, new_pos, new_vel,
+    positions, velocities, codes, counts, w_first, w_second, w_read, w_out, fresh_pos, fresh_vel,
+    pos, vel_in, fx, place, geo, unit, basis, hid, wgt, got, agg, slopes, edge, lhs, hot_t,
+    forces, tail, first, second, read3, read_t3, out_col, own_sem, load_sem, send_sem, recv_sem,
 ):
     s = lax.axis_index("shock")
     t = lax.axis_index("trans")
@@ -344,68 +370,109 @@
         pl.semaphore_signal(
             barrier, inc=1, device_id=at(ds, dt), device_id_type=pl.DeviceIdType.MESH
         )
-    own = pltpu.make_async_copy(features.at[:, 0], fx.at[pl.ds(1, 2), 1], own_sem)
+    own = pltpu.make_async_copy(features.at[:, 0], fx.at[pl.ds(1, 2), 0], own_sem)
+    loads = [
+        pltpu.make_async_copy(src, dst, load_sem.at[i])
+        for i, (src, dst) in enumerate(
+            (
+                (codes_in, codes),
+                (positions_in, positions),
+                (counts_in, counts),
+                (w_first_in, w_first),
+                (w_second_in, w_second),
+                (w_read_in, w_read),
+                (w_out_in, w_out),
+                (velocities_in, velocities),
+                (fresh_pos_in, fresh_pos),
+                (fresh_vel_in, fresh_vel),
+                (positions_in, pos.at[pl.ds(1, 2), 0]),
+            )
+        )
+    ]
     own.start()
-    pos[1:3, 1] = positions[:, 0]
+    for load in loads:
+        load.start()
+    loads[0].wait()
+    for r in range(2):
+        places(r, way, codes, place)
     pl.semaphore_wait(barrier, 10)
 
     flights = {}
+
+    def role(dt):
+        return 0 if dt == 0 else (3 - dt * way) // 2
+
     for i, (ds, dt) in enumerate(AROUND):
         if ds == 0:
-            src, dst = positions.at[:, 0], pos.at[pl.ds(1, 2), 1 - dt]
+            src, dst = positions_in, pos.at[pl.ds(1, 2), role(dt)]
         elif ds == 1:
-            src, dst = positions.at[1, 0], pos.at[0, 1 - dt]
+            src, dst = positions_in.at[1], pos.at[0, role(dt)]
         else:
-            src, dst = positions.at[0, 0], pos.at[3, 1 - dt]
+            src, dst = positions_in.at[0], pos.at[3, role(dt)]
         flights[POS + i] = copy(POS + i, src, dst, at(ds, dt))
-    flights[VEL] = copy(VEL, velocities.at[0, 0], vel_in, at(-1, 0))
-    near, far = 1 + way, 1 - way
-    for i in range(2):
-        flights[OWN + i] = copy(OWN + i, features.at[i, 0], fx.at[1 + i, far], at(0, way))
+    flights[VEL] = copy(VEL, velocities_in.at[0], vel_in, at(-1, 0))
     chip_row, chip_ghost = 1 - core, 3 * core
     off_row, off_ghost = core, 3 * (1 - core)
-    flights[CHIP] = copy(CHIP, features.at[chip_row, 0], fx.at[chip_ghost, 1], at(-out_way, 0))
-    flights[OFF] = copy(OFF, features.at[off_row, 0], fx.at[off_ghost, 1], at(out_way, 0))
-    flights[CORNER] = copy(
-        CORNER, features.at[off_row, 0], fx.at[off_ghost, far], at(out_way, way)
-    )
+    order = (chip_row, off_row)
+    for i in range(2):
+        flights[OWN + i] = copy(OWN + i, features.at[order[i], 0], fx.at[1 + order[i], 1], at(0, way))
+    flights[CHIP] = copy(CHIP, features.at[chip_row, 0], fx.at[chip_ghost, 0], at(-out_way, 0))
+    flights[OFF] = copy(OFF, features.at[off_row, 0], fx.at[off_ghost, 0], at(out_way, 0))
+    flights[CORNER] = copy(CORNER, features.at[off_row, 0], fx.at[off_ghost, 1], at(out_way, way))
     for k in list(range(POS, POS + 8)) + [OWN, OWN + 1, CORNER, OFF, CHIP, VEL]:
         flights[k].start()
-    my_chip_ghost, my_off_ghost = 3 * (1 - core), 3 * core
+    my_off_ghost = 3 * core
     for i in range(2):
-        flights[FAR + i] = copy(
-            FAR + i, fx.at[1 + i, near], fx.at[1 + i, far], at(0, 2 * way)
-        )
+        row = 1 + order[i]
+        flights[FAR + i] = copy(FAR + i, fx.at[row, 1], fx.at[row, 2], at(0, 2 * way))
     flights[FAR_CORNER] = copy(
-        FAR_CORNER, fx.at[my_off_ghost, near], fx.at[my_off_ghost, far], at(0, 2 * way)
+        FAR_CORNER, fx.at[my_off_ghost, 1], fx.at[my_off_ghost, 2], at(0, 2 * way)
     )
     flights[NEAR_CHIP] = copy(
-        NEAR_CHIP, fx.at[1 + chip_row, near], fx.at[chip_ghost, near], at(-out_way, 0)
+        NEAR_CHIP, fx.at[1 + chip_row, 1], fx.at[chip_ghost, 1], at(-out_way, 0)
     )
     flights[FAR_CHIP] = copy(
-        FAR_CHIP, fx.at[1 + chip_row, far], fx.at[chip_ghost, far], at(-out_way, 0)
+        FAR_CHIP, fx.at[1 + chip_row, 2], fx.at[chip_ghost, 2], at(-out_way, 0)
     )
 
-    first[...] = jnp.concatenate([stack(w_first[...], 1), jnp.zeros((64, 8), BF16)], axis=1)
-    second[...] = stack(w_second[...], 1)
-    read3[...] = stack(w_read[...], 1)
-    read_t3[...] = stack(w_read[...], 0)
+    def gather_stage(r, stage):
+        def gather_step(step, carry):
+            gather(r, stage, step, place, fx, got)
+            return carry
+
+        lax.fori_loop(0, 12, gather_step, 0, unroll=4)
+
+    own.wait()
+    for r in range(2):
+        gather_stage(r, 0)
+
+    for load in loads[1:]:
+        load.wait()
+    first[...] = jnp.concatenate([stack(w_first[...].T, 1), jnp.zeros((64, 8), BF16)], axis=1)
+    second[...] = stack(w_second[...].T, 1)
+    read3[...] = stack(w_read[...].T, 1)
+    read_t3[...] = stack(w_read[...], 1)
     col = jnp.broadcast_to(w_out[...], (128, 128)).T
     out_col[...] = jnp.concatenate([col, col], axis=1)
+    flights[OWN].wait_recv()
+    flights[FAR].start()
+    flights[NEAR_CHIP].start()
+    for r in range(2):
+        hot_rows(r, place, hot_t)
 
     for k in range(POS, POS + 8):
         flights[k].wait_recv()
 
     @pl.when(s == 0)
     def _():
-        pos[0] = jnp.zeros((3, 3, 128), F32)
+        pos[0] = jnp.zeros((3, 3, 1, 128), F32)
 
     @pl.when(s == ns - 1)
     def _():
-        pos[3] = jnp.zeros((3, 3, 128), F32)
-
-    for r in range(2):
-        geometry(r, pos, codes, counts, geo, unit)
+        pos[3] = jnp.zeros((3, 3, 1, 128), F32)
+
+    for r in range(2):
+        geometry(r, pos, codes, place, counts, geo, unit)
 
     def radial_steps(lo, hi):
         def radial_step(step, carry):
@@ -415,41 +482,37 @@
         lax.fori_loop(lo, hi, radial_step, 0)
 
     total = 48 // SPAN
-    radial_steps(0, total // 4)
-    for i in range(2):
-        flights[OWN + i].wait_recv()
-        flights[FAR + i].start()
-    flights[NEAR_CHIP].start()
-    radial_steps(total // 4, total // 2)
+    radial_steps(0, total // 2)
+    flights[OWN + 1].wait_recv()
+    flights[FAR + 1].start()
+    radial_steps(total // 2, total)
+    flights[FAR].wait_recv()
+    flights[FAR_CHIP].start()
     flights[CORNER].wait_recv()
     flights[FAR_CORNER].start()
-    radial_steps(total // 2, total)
-    for i in range(2):
-        flights[FAR + i].wait_recv()
-    flights[FAR_CHIP].start()
-    own.wait()
-    for k in (CHIP, OFF, NEAR_CHIP, FAR_CORNER, FAR_CHIP, VEL):
+    for k in (CHIP, OFF, NEAR_CHIP):
         flights[k].wait_recv()
-    for k in range(TAIL):
-        flights[k].wait_send()
-
-    @pl.when(s == 0)
-    def _():
-        fx[0] = jnp.zeros((3, 576, 128), BF16)
-
-    @pl.when(s == ns - 1)
-    def _():
-        fx[3] = jnp.zeros((3, 576, 128), BF16)
-
-    for r in range(2):
-        for b in range(9):
-            window[r, :, 128 * b : 128 * b + 128] = fx[r + b // 3, b % 3]
-
-    def gather_step(step, carry):
-        gather(step, codes, window, got)
-        return carry
-
-    lax.fori_loop(0, 24, gather_step, 0)
+    flights[FAR_CORNER].wait_send()
+    blank = jnp.zeros((576, 128), BF16)
+
+    def close(role):
+        @pl.when(s == 0)
+        def _():
+            fx[0, role] = blank
+
+        @pl.when(s == ns - 1)
+        def _():
+            fx[3, role] = blank
+
+    close(0)
+    close(1)
+    gather_stage(0, 1)
+    gather_stage(1, 1)
+    for k in (FAR + 1, FAR_CORNER, FAR_CHIP):
+        flights[k].wait_recv()
+    close(2)
+    for r in range(2):
+        gather_stage(r, 2)
 
     def aggregate_step(step, carry):
         aggregate(step, geo, wgt, got, agg)
@@ -462,28 +525,30 @@
         backward(step, geo, wgt, got, agg, slopes)
         return carry
 
-    lax.fori_loop(0, 48, backward_step, 0)
+    lax.fori_loop(0, 48, backward_step, 0, unroll=2)
     forces[...] = jnp.zeros_like(forces)
     for r in range(2):
         centre = edge_forces(r, geo, unit, slopes, edge)
-        scatter(r, codes, edge, lhs, hot, centre, forces)
+        scatter(r, place, edge, lhs, hot_t, centre, forces)
 
     for i, (ds, dt) in enumerate(BACK):
-        src = forces.at[1 + dt, pl.ds(2 if ds == 0 else 0, 2)]
+        src = forces.at[role(dt), pl.ds(2 if ds == 0 else 0, 2)]
         flights[TAIL + i] = copy(TAIL + i, src, tail.at[i], at(ds, dt))
         flights[TAIL + i].start()
+    for k in list(range(FAR_CORNER)):
+        flights[k].wait_send()
+    flights[VEL].wait_recv()
     for i in range(5):
         flights[TAIL + i].wait_recv()
     front = s == ns - 1
     above = tail[2] + tail[3] + tail[4]
-    force = forces[1, 2:4] + tail[0] + tail[1] + jnp.where(front, 0.0, above)
-    force = force[:, 0:3]
-    vel = velocities[1, 0] + KICK_FACTOR * force[0]
-    new_vel[0, 0] = vel
-    new_pos[0, 0] = positions[1, 0] + MOVE_FACTOR * vel
+    force = forces[0, 2:4] + tail[0] + tail[1] + jnp.where(front, 0.0, above)
+    vel = velocities[1] + KICK_FACTOR * force[0]
+    new_vel[0] = vel
+    new_pos[0] = positions[1] + MOVE_FACTOR * vel
     vel = vel_in[...] + KICK_FACTOR * force[1]
-    new_vel[1, 0] = jnp.where(front, fresh_vel[0], vel)
-    new_pos[1, 0] = jnp.where(front, fresh_pos[0], pos[3, 1] + MOVE_FACTOR * vel)
+    new_vel[1] = jnp.where(front, fresh_vel[...], vel)
+    new_pos[1] = jnp.where(front, fresh_pos[...], pos[3, 0] + MOVE_FACTOR * vel)
     for i in range(5):
         flights[TAIL + i].wait_send()
 
@@ -494,39 +559,50 @@
 ):
     vmem = pl.BlockSpec(memory_space=pltpu.VMEM)
     whole = pl.BlockSpec(memory_space=pl.ANY)
-    return pl.pallas_call(
+    energies, new_pos, new_vel = pl.pallas_call(
         step_kernel,
         out_shape=(
             jax.ShapeDtypeStruct((2, 1, 128), F32),
-            jax.ShapeDtypeStruct((2, 1, 3, 128), F32),
-            jax.ShapeDtypeStruct((2, 1, 3, 128), F32),
+            jax.ShapeDtypeStruct((2, 3, 1, 128), F32),
+            jax.ShapeDtypeStruct((2, 3, 1, 128), F32),
         ),
-        in_specs=[vmem, vmem, whole] + [vmem] * 8,
+        in_specs=[whole] * 11,
         out_specs=(vmem, vmem, vmem),
         scratch_shapes=[
-            pltpu.VMEM((4, 3, 3, 128), F32),
-            pltpu.VMEM((3, 128), F32),
+            pltpu.VMEM((2, 3, 1, 128), F32),
+            pltpu.VMEM((2, 3, 1, 128), F32),
+            pltpu.VMEM((2, 1, 24, 128), jnp.int32),
+            pltpu.VMEM((2, 1, 128), jnp.int32),
+            pltpu.VMEM((8, 64), F32),
+            pltpu.VMEM((64, 192), F32),
+            pltpu.VMEM((192, 128), F32),
+            pltpu.VMEM((1, 128), F32),
+            pltpu.VMEM((3, 1, 128), F32),
+            pltpu.VMEM((3, 1, 128), F32),
+            pltpu.VMEM((4, 3, 3, 1, 128), F32),
+            pltpu.VMEM((3, 1, 128), F32),
             pltpu.VMEM((4, 3, 576, 128), BF16),
+            pltpu.VMEM((2, 24, 128), jnp.int32),
             pltpu.VMEM((2, GEO, 24, 128), F32),
             pltpu.VMEM((2, 3, 24, 128), F32),
             pltpu.VMEM((32, 256 * SPAN), BF16),
             pltpu.VMEM((192, 256 * SPAN), BF16),
             pltpu.VMEM((2, 24, 2, 192, 128), F32),
-            pltpu.VMEM((2, 576, 1152), BF16),
             pltpu.VMEM((2, 24, 576, 128), F32),
             pltpu.VMEM((2, 9, 64, 128), F32),
             pltpu.VMEM((2, 9, 24, 128), F32),
             pltpu.VMEM((3, 24, 128), F32),
             pltpu.VMEM((80, 3072), BF16),
-            pltpu.VMEM((128, 3072), BF16),
-            pltpu.VMEM((3, 4, 8, 128), F32),
-            pltpu.VMEM((5, 2, 8, 128), F32),
+            pltpu.VMEM((2, 3072, 128), BF16),
+            pltpu.VMEM((3, 4, 3, 1, 128), F32),
+            pltpu.VMEM((5, 2, 3, 1, 128), F32),
             pltpu.VMEM((64, 32), BF16),
             pltpu.VMEM((192, 192), BF16),
             pltpu.VMEM((128, 576), BF16),
-            pltpu.VMEM((384, 192), BF16),
+            pltpu.VMEM((192, 384), BF16),
             pltpu.VMEM((128, 256), F32),
             pltpu.SemaphoreType.DMA,
+            pltpu.SemaphoreType.DMA((11,)),
             pltpu.SemaphoreType.DMA((COPIES,)),
             pltpu.SemaphoreType.DMA((COPIES,)),
         ],
@@ -535,9 +611,11 @@
         ),
         name="step",
     )(
-        positions, velocities, features, neighbours, counts, w_first, w_second, w_read,
-        w_out[None], fresh_positions, fresh_velocities,
+        positions.transpose(0, 2, 1, 3), velocities.transpose(0, 2, 1, 3), features, neighbours,
+        counts, w_first.T, w_second.T, w_read.T, w_out[None],
+        fresh_positions.transpose(1, 0, 2), fresh_velocities.transpose(1, 0, 2),
     )
+    return energies, new_pos.transpose(0, 2, 1, 3), new_vel.transpose(0, 2, 1, 3)
 
 
 def solution(mesh):

time: 69 us -> 52.9 us (0.77); the launches traced: 67.6 us -> 52.7 us
  Pallas kernels: 58.3 us -> 49.6 us
  local copies, waits for them, and re-layouts: 8.68 us -> 2.47 us
    pallas_call x1, Pallas kernels: 58.3 us -> 49.6 us  [local(): pl.pallas_call(step_kernel, out_shape=(jax.ShapeDtypeStruct((2, 1, 128),...]
    unnamed x26 -> x9, local copies, waits for them, and re-layouts: 7.52 us -> 2.47 us
    pallas_call x2 -> x0, local copies, waits for them, and re-layouts: 1.16 us -> none  [local(): pl.pallas_call(step_kernel, out_shape=(jax.ShapeDtypeStruct((2, 1, 128),...]
where the time goes in v3:
time: 52.9 us; the launch traced here: 52.7 us
  Pallas kernels  49.6 us (94%)
  local copies, waits for them, and re-layouts  2.47 us (5%)
  between operations  0.66 us (1%)
    pallas_call x1, Pallas kernels, local(): pl.pallas_call(step_kernel, out_shape=(jax.ShapeDtypeStruct((2, 1, 128),...  49.6 us
    unnamed x9, local copies, waits for them, and re-layouts  2.47 us

profile of v3, /device:TPU:1, one launch (start us, length us, event | category | flops | bytes accessed | tf_op | source)
XLA Modules:
  0.0 52.7 jit_solution(17723421568971888717)
XLA Ops:
  0.6 49.6 %step.1 = (f32[2,1,128]{2,1,0:T(1,128)}, f32[2,3,1,128]{3,2,1,0:T(1,128)}, f32[2,3,1,128]{3,2,1,0:T(1,128)}) custom-call(f32[2,3,1,128]{3,2,1,0:T(1,128)} %bitcast.13, f32[2,3,1,128]{3,2,1,0:T(1,128)} %bitcast.14, bf16[2,1,576,128]{3,2,1,0:T(8,128)(2,1)} %features.1, s32[2,1,24,128]{3,2,1,0:T(8,128)} %codes_in.1, s32[2,1,128]{2,1,0:T(1,128)} %counts_in.1, ...), custom_call_target="tpu_custom_call" | custom-call | tf_op jit(solution)/shard_map/step/pallas_call | solution.py:562
  50.3 0.0 copy-start.2
  50.3 0.0 copy-start.1
  50.3 0.6 %copy-done.2 = f32[2,1,128]{2,1,0:T(1,128)S(1)} copy-done((f32[2,1,128]{2,1,0:T(1,128)S(1)}, f32[2,1,128]{2,1,0:T(1,128)}, u32[]{:S(2)}) %copy-start.2) | copy-done | bytes 1048
  50.9 0.6 %copy.17 = f32[2,1,128]{2,1,0:T(1,128)} copy(f32[2,1,128]{2,1,0:T(1,128)S(1)} %copy-done.2) | data formatting | bytes 2048
  51.5 0.0 copy-done.1
  51.5 0.0 copy-start
  51.5 0.6 %copy.18 = f32[2,1,3,128]{3,1,2,0:T(1,128)} copy(f32[2,1,3,128]{3,1,2,0:T(1,128)S(1)} %bitcast.16) | data formatting | bytes 6144
  52.1 0.1 copy-done
  52.2 0.6 %copy.19 = f32[2,1,3,128]{3,1,2,0:T(1,128)} copy(f32[2,1,3,128]{3,1,2,0:T(1,128)S(1)} %bitcast.15) | data formatting | bytes 6144
Async XLA Ops:
  50.3 0.7 %copy-start.2 = (f32[2,1,128]{2,1,0:T(1,128)S(1)}, f32[2,1,128]{2,1,0:T(1,128)}, u32[]{:S(2)}) copy-start(f32[2,1,128]{2,1,0:T(1,128)} %get-tuple-element.12) | copy-start | bytes 3076
  50.3 1.2 %copy-start.1 = (f32[2,3,1,128]{3,2,1,0:T(1,128)S(1)}, f32[2,3,1,128]{3,2,1,0:T(1,128)}, u32[]{:S(2)}) copy-start(f32[2,3,1,128]{3,2,1,0:T(1,128)} %get-tuple-element.7) | copy-start | bytes 9220
  51.5 0.7 %copy-start = (f32[2,3,1,128]{3,2,1,0:T(1,128)S(1)}, f32[2,3,1,128]{3,2,1,0:T(1,128)}, u32[]{:S(2)}) copy-start(f32[2,3,1,128]{3,2,1,0:T(1,128)} %get-tuple-element.8) | copy-start | bytes 9220

commit v4 on v3

--- a/solution.py
+++ b/solution.py
@@ -324,15 +324,15 @@
 POS = 0
 VEL = 8
 OWN = 9
-CHIP = 11
-OFF = 12
-CORNER = 13
-FAR = 14
-NEAR_CHIP = 16
-FAR_CHIP = 17
-FAR_CORNER = 18
-TAIL = 19
-COPIES = 24
+CHIP = 13
+OFF = 14
+CORNER = 15
+FAR = 17
+NEAR_CHIP = 21
+FAR_CHIP = 22
+FAR_CORNER = 23
+TAIL = 25
+COPIES = 30
 AROUND = ((-1, -1), (-1, 0), (-1, 1), (0, -1), (0, 1), (1, -1), (1, 0), (1, 1))
 BACK = ((0, 1), (0, -1), (-1, 1), (-1, 0), (-1, -1))
 
@@ -392,9 +392,6 @@
     own.start()
     for load in loads:
         load.start()
-    loads[0].wait()
-    for r in range(2):
-        places(r, way, codes, place)
     pl.semaphore_wait(barrier, 10)
 
     flights = {}
@@ -414,20 +411,27 @@
     chip_row, chip_ghost = 1 - core, 3 * core
     off_row, off_ghost = core, 3 * (1 - core)
     order = (chip_row, off_row)
-    for i in range(2):
-        flights[OWN + i] = copy(OWN + i, features.at[order[i], 0], fx.at[1 + order[i], 1], at(0, way))
+    my_off_ghost = 3 * core
+    for i in range(4):
+        row, half = 1 + order[i // 2], pl.ds(288 * (i % 2), 288)
+        flights[OWN + i] = copy(
+            OWN + i, features.at[row - 1, 0, half], fx.at[row, 1, half], at(0, way)
+        )
+        flights[FAR + i] = copy(
+            FAR + i, fx.at[row, 1, half], fx.at[row, 2, half], at(0, 2 * way)
+        )
     flights[CHIP] = copy(CHIP, features.at[chip_row, 0], fx.at[chip_ghost, 0], at(-out_way, 0))
     flights[OFF] = copy(OFF, features.at[off_row, 0], fx.at[off_ghost, 0], at(out_way, 0))
-    flights[CORNER] = copy(CORNER, features.at[off_row, 0], fx.at[off_ghost, 1], at(out_way, way))
-    for k in list(range(POS, POS + 8)) + [OWN, OWN + 1, CORNER, OFF, CHIP, VEL]:
+    for i in range(2):
+        half = pl.ds(288 * i, 288)
+        flights[CORNER + i] = copy(
+            CORNER + i, features.at[off_row, 0, half], fx.at[off_ghost, 1, half], at(out_way, way)
+        )
+        flights[FAR_CORNER + i] = copy(
+            FAR_CORNER + i, fx.at[my_off_ghost, 1, half], fx.at[my_off_ghost, 2, half], at(0, 2 * way)
+        )
+    for k in [OWN, *range(POS, POS + 8), *range(OWN + 1, OWN + 4), CHIP, CORNER, CORNER + 1, OFF, VEL]:
         flights[k].start()
-    my_off_ghost = 3 * core
-    for i in range(2):
-        row = 1 + order[i]
-        flights[FAR + i] = copy(FAR + i, fx.at[row, 1], fx.at[row, 2], at(0, 2 * way))
-    flights[FAR_CORNER] = copy(
-        FAR_CORNER, fx.at[my_off_ghost, 1], fx.at[my_off_ghost, 2], at(0, 2 * way)
-    )
     flights[NEAR_CHIP] = copy(
         NEAR_CHIP, fx.at[1 + chip_row, 1], fx.at[chip_ghost, 1], at(-out_way, 0)
     )
@@ -440,11 +444,19 @@
             gather(r, stage, step, place, fx, got)
             return carry
 
-        lax.fori_loop(0, 12, gather_step, 0, unroll=4)
-
+        lax.fori_loop(0, 12, gather_step, 0, unroll=6)
+
+    def pass_on(k, to):
+        flights[k].wait_recv()
+        flights[to].start()
+
+    loads[0].wait()
+    for r in range(2):
+        places(r, way, codes, place)
     own.wait()
-    for r in range(2):
-        gather_stage(r, 0)
+    gather_stage(0, 0)
+    gather_stage(1, 0)
+    pass_on(OWN, FAR)
 
     for load in loads[1:]:
         load.wait()
@@ -454,11 +466,10 @@
     read_t3[...] = stack(w_read[...], 1)
     col = jnp.broadcast_to(w_out[...], (128, 128)).T
     out_col[...] = jnp.concatenate([col, col], axis=1)
-    flights[OWN].wait_recv()
-    flights[FAR].start()
+    hot_rows(0, place, hot_t)
+    pass_on(OWN + 1, FAR + 1)
     flights[NEAR_CHIP].start()
-    for r in range(2):
-        hot_rows(r, place, hot_t)
+    hot_rows(1, place, hot_t)
 
     for k in range(POS, POS + 8):
         flights[k].wait_recv()
@@ -474,25 +485,25 @@
     for r in range(2):
         geometry(r, pos, codes, place, counts, geo, unit)
 
-    def radial_steps(lo, hi):
-        def radial_step(step, carry):
-            radial(step, geo, first[...], second[...], basis, hid, wgt)
-            return carry
-
-        lax.fori_loop(lo, hi, radial_step, 0)
-
-    total = 48 // SPAN
-    radial_steps(0, total // 2)
-    flights[OWN + 1].wait_recv()
-    flights[FAR + 1].start()
-    radial_steps(total // 2, total)
+    def radial_step(step, carry):
+        radial(step, geo, first[...], second[...], basis, hid, wgt)
+        return carry
+
+    pass_on(OWN + 2, FAR + 2)
+    lax.fori_loop(0, 24 // SPAN, radial_step, 0)
+    pass_on(OWN + 3, FAR + 3)
+    lax.fori_loop(24 // SPAN, 48 // SPAN, radial_step, 0)
     flights[FAR].wait_recv()
+    flights[FAR + 1].wait_recv()
     flights[FAR_CHIP].start()
-    flights[CORNER].wait_recv()
-    flights[FAR_CORNER].start()
-    for k in (CHIP, OFF, NEAR_CHIP):
-        flights[k].wait_recv()
-    flights[FAR_CORNER].wait_send()
+    pass_on(CORNER, FAR_CORNER)
+    flights[CHIP].wait_recv()
+    flights[NEAR_CHIP].wait_recv()
+    gather_stage(1 - core, 1)
+    pass_on(CORNER + 1, FAR_CORNER + 1)
+    flights[OFF].wait_recv()
+    for i in range(2):
+        flights[FAR_CORNER + i].wait_send()
     blank = jnp.zeros((576, 128), BF16)
 
     def close(role):
@@ -506,13 +517,14 @@
 
     close(0)
     close(1)
-    gather_stage(0, 1)
-    gather_stage(1, 1)
-    for k in (FAR + 1, FAR_CORNER, FAR_CHIP):
+    gather_stage(core, 1)
+    for k in (FAR + 2, FAR + 3, FAR_CHIP):
         flights[k].wait_recv()
+    gather_stage(1 - core, 2)
+    for i in range(2):
+        flights[FAR_CORNER + i].wait_recv()
     close(2)
-    for r in range(2):
-        gather_stage(r, 2)
+    gather_stage(core, 2)
 
     def aggregate_step(step, carry):
         aggregate(step, geo, wgt, got, agg)
@@ -525,7 +537,7 @@
         backward(step, geo, wgt, got, agg, slopes)
         return carry
 
-    lax.fori_loop(0, 48, backward_step, 0, unroll=2)
+    lax.fori_loop(0, 48, backward_step, 0, unroll=4)
     forces[...] = jnp.zeros_like(forces)
     for r in range(2):
         centre = edge_forces(r, geo, unit, slopes, edge)

time: 52.9 us -> 48.5 us (0.917)
  Pallas kernels: 49.6 us -> 45.2 us
    pallas_call x1, Pallas kernels: 49.6 us -> 45.2 us  [local(): pl.pallas_call(step_kernel, out_shape=(jax.ShapeDtypeStruct((2, 1, 128),...]
where the time goes in v4:
time: 48.5 us; the launch traced here: 48.3 us
  Pallas kernels  45.2 us (93%)
  local copies, waits for them, and re-layouts  2.47 us (5%)
  between operations  0.66 us (1%)
    pallas_call x1, Pallas kernels, local(): pl.pallas_call(step_kernel, out_shape=(jax.ShapeDtypeStruct((2, 1, 128),...  45.2 us
    unnamed x9, local copies, waits for them, and re-layouts  2.47 us

profile of v4, /device:TPU:1, one launch (start us, length us, event | category | flops | bytes accessed | tf_op | source)
XLA Modules:
  0.0 48.3 jit_solution(4884198329875355175)
XLA Ops:
  0.6 45.2 %step.1 = (f32[2,1,128]{2,1,0:T(1,128)}, f32[2,3,1,128]{3,2,1,0:T(1,128)}, f32[2,3,1,128]{3,2,1,0:T(1,128)}) custom-call(f32[2,3,1,128]{3,2,1,0:T(1,128)} %bitcast.13, f32[2,3,1,128]{3,2,1,0:T(1,128)} %bitcast.14, bf16[2,1,576,128]{3,2,1,0:T(8,128)(2,1)} %features.1, s32[2,1,24,128]{3,2,1,0:T(8,128)} %codes_in.1, s32[2,1,128]{2,1,0:T(1,128)} %counts_in.1, ...), custom_call_target="tpu_custom_call" | custom-call | tf_op jit(solution)/shard_map/step/pallas_call | solution.py:574
  45.8 0.0 copy-start.2
  45.8 0.0 copy-start.1
  45.8 0.6 %copy-done.2 = f32[2,1,128]{2,1,0:T(1,128)S(1)} copy-done((f32[2,1,128]{2,1,0:T(1,128)S(1)}, f32[2,1,128]{2,1,0:T(1,128)}, u32[]{:S(2)}) %copy-start.2) | copy-done | bytes 1048
  46.5 0.6 %copy.17 = f32[2,1,128]{2,1,0:T(1,128)} copy(f32[2,1,128]{2,1,0:T(1,128)S(1)} %copy-done.2) | data formatting | bytes 2048
  47.0 0.0 copy-done.1
  47.1 0.0 copy-start
  47.1 0.6 %copy.18 = f32[2,1,3,128]{3,1,2,0:T(1,128)} copy(f32[2,1,3,128]{3,1,2,0:T(1,128)S(1)} %bitcast.16) | data formatting | bytes 6144
  47.6 0.1 copy-done
  47.7 0.6 %copy.19 = f32[2,1,3,128]{3,1,2,0:T(1,128)} copy(f32[2,1,3,128]{3,1,2,0:T(1,128)S(1)} %bitcast.15) | data formatting | bytes 6144
Async XLA Ops:
  45.8 0.7 %copy-start.2 = (f32[2,1,128]{2,1,0:T(1,128)S(1)}, f32[2,1,128]{2,1,0:T(1,128)}, u32[]{:S(2)}) copy-start(f32[2,1,128]{2,1,0:T(1,128)} %get-tuple-element.12) | copy-start | bytes 3076
  45.8 1.2 %copy-start.1 = (f32[2,3,1,128]{3,2,1,0:T(1,128)S(1)}, f32[2,3,1,128]{3,2,1,0:T(1,128)}, u32[]{:S(2)}) copy-start(f32[2,3,1,128]{3,2,1,0:T(1,128)} %get-tuple-element.7) | copy-start | bytes 9220
  47.1 0.7 %copy-start = (f32[2,3,1,128]{3,2,1,0:T(1,128)S(1)}, f32[2,3,1,128]{3,2,1,0:T(1,128)}, u32[]{:S(2)}) copy-start(f32[2,3,1,128]{3,2,1,0:T(1,128)} %get-tuple-element.8) | copy-start | bytes 9220

commit v5 on v4

--- a/solution.py
+++ b/solution.py
@@ -439,12 +439,12 @@
         FAR_CHIP, fx.at[1 + chip_row, 2], fx.at[chip_ghost, 2], at(-out_way, 0)
     )
 
-    def gather_stage(r, stage):
+    def gather_stage(r, stage, first_step=0, last_step=12):
         def gather_step(step, carry):
             gather(r, stage, step, place, fx, got)
             return carry
 
-        lax.fori_loop(0, 12, gather_step, 0, unroll=6)
+        lax.fori_loop(first_step, last_step, gather_step, 0, unroll=6)
 
     def pass_on(k, to):
         flights[k].wait_recv()
@@ -499,8 +499,9 @@
     pass_on(CORNER, FAR_CORNER)
     flights[CHIP].wait_recv()
     flights[NEAR_CHIP].wait_recv()
-    gather_stage(1 - core, 1)
+    gather_stage(1 - core, 1, 0, 6)
     pass_on(CORNER + 1, FAR_CORNER + 1)
+    gather_stage(1 - core, 1, 6, 12)
     flights[OFF].wait_recv()
     for i in range(2):
         flights[FAR_CORNER + i].wait_send()
@@ -521,16 +522,20 @@
     for k in (FAR + 2, FAR + 3, FAR_CHIP):
         flights[k].wait_recv()
     gather_stage(1 - core, 2)
+
+    def aggregate_row(r):
+        def aggregate_step(step, carry):
+            aggregate(r * (64 // TILE) + step, geo, wgt, got, agg)
+            return carry
+
+        lax.fori_loop(0, 64 // TILE, aggregate_step, 0)
+
+    aggregate_row(1 - core)
     for i in range(2):
         flights[FAR_CORNER + i].wait_recv()
     close(2)
     gather_stage(core, 2)
-
-    def aggregate_step(step, carry):
-        aggregate(step, geo, wgt, got, agg)
-        return carry
-
-    lax.fori_loop(0, 2 * (64 // TILE), aggregate_step, 0)
+    aggregate_row(core)
     readout(agg, read3[...], read_t3[...], out_col[...], energies)
 
     def backward_step(step, carry):
@@ -574,9 +579,9 @@
     energies, new_pos, new_vel = pl.pallas_call(
         step_kernel,
         out_shape=(
-            jax.ShapeDtypeStruct((2, 1, 128), F32),
-            jax.ShapeDtypeStruct((2, 3, 1, 128), F32),
-            jax.ShapeDtypeStruct((2, 3, 1, 128), F32),
+            pltpu.VMEM((2, 1, 128), F32),
+            pltpu.VMEM((2, 3, 1, 128), F32),
+            pltpu.VMEM((2, 3, 1, 128), F32),
         ),
         in_specs=[whole] * 11,
         out_specs=(vmem, vmem, vmem),

time: 48.5 us -> 46.8 us (0.965)
  Pallas kernels: 45.2 us -> 44.3 us
  local copies, waits for them, and re-layouts: 2.47 us -> 1.72 us
    pallas_call x1, Pallas kernels: 45.2 us -> 44.3 us  [local(): pl.pallas_call(step_kernel, out_shape=(pltpu.VMEM((2, 1, 128), F32), pltp...]
    unnamed x9 -> x3, local copies, waits for them, and re-layouts: 2.47 us -> 1.72 us
where the time goes in v5:
time: 46.8 us; the launch traced here: 46.7 us
  Pallas kernels  44.3 us (95%)
  local copies, waits for them, and re-layouts  1.72 us (4%)
  between operations  0.64 us (1%)
    pallas_call x1, Pallas kernels, local(): pl.pallas_call(step_kernel, out_shape=(pltpu.VMEM((2, 1, 128), F32), pltp...  44.3 us
    unnamed x3, local copies, waits for them, and re-layouts  1.72 us

profile of v5, /device:TPU:1, one launch (start us, length us, event | category | flops | bytes accessed | tf_op | source)
XLA Modules:
  0.0 46.7 jit_solution(9632371419058651073)
XLA Ops:
  0.6 44.3 %step.1 = (f32[2,1,128]{2,1,0:T(1,128)S(1)}, f32[2,3,1,128]{3,2,1,0:T(1,128)S(1)}, f32[2,3,1,128]{3,2,1,0:T(1,128)S(1)}) custom-call(f32[2,3,1,128]{3,2,1,0:T(1,128)} %bitcast.15, f32[2,3,1,128]{3,2,1,0:T(1,128)} %bitcast.16, bf16[2,1,576,128]{3,2,1,0:T(8,128)(2,1)} %features.1, s32[2,1,24,128]{3,2,1,0:T(8,128)} %codes_in.1, s32[2,1,128]{2,1,0:T(1,128)} %counts_in.1, ...), custom_call_target="tpu_custom_call" | custom-call | tf_op jit(solution)/shard_map/step/pallas_call | solution.py:579
  45.0 0.6 %copy.17 = f32[2,1,128]{2,1,0:T(1,128)} copy(f32[2,1,128]{2,1,0:T(1,128)S(1)} %get-tuple-element.9) | data formatting | bytes 2048
  45.6 0.6 %copy.18 = f32[2,1,3,128]{3,1,2,0:T(1,128)} copy(f32[2,1,3,128]{3,1,2,0:T(1,128)S(1)} %bitcast.11) | data formatting | bytes 6144
  46.1 0.6 %copy.19 = f32[2,1,3,128]{3,1,2,0:T(1,128)} copy(f32[2,1,3,128]{3,1,2,0:T(1,128)S(1)} %bitcast.10) | data formatting | bytes 6144

commit v6 on v5

--- a/solution.py
+++ b/solution.py
@@ -444,7 +444,7 @@
             gather(r, stage, step, place, fx, got)
             return carry
 
-        lax.fori_loop(first_step, last_step, gather_step, 0, unroll=6)
+        lax.fori_loop(first_step, last_step, gather_step, 0, unroll=last_step - first_step)
 
     def pass_on(k, to):
         flights[k].wait_recv()

time: 46.8 us -> 46.5 us (level)
  no operation moved by 1% of the time
where the time goes in v6:
time: 46.5 us; the launch traced here: 46.4 us
  Pallas kernels  44 us (95%)
  local copies, waits for them, and re-layouts  1.72 us (4%)
  between operations  0.64 us (1%)
    pallas_call x1, Pallas kernels, local(): pl.pallas_call(step_kernel, out_shape=(pltpu.VMEM((2, 1, 128), F32), pltp...  44 us
    unnamed x3, local copies, waits for them, and re-layouts  1.72 us

profile of v6, /device:TPU:1, one launch (start us, length us, event | category | flops | bytes accessed | tf_op | source)
XLA Modules:
  0.0 46.4 jit_solution(17869081994685806043)
XLA Ops:
  0.6 44.0 %step.1 = (f32[2,1,128]{2,1,0:T(1,128)S(1)}, f32[2,3,1,128]{3,2,1,0:T(1,128)S(1)}, f32[2,3,1,128]{3,2,1,0:T(1,128)S(1)}) custom-call(f32[2,3,1,128]{3,2,1,0:T(1,128)} %bitcast.15, f32[2,3,1,128]{3,2,1,0:T(1,128)} %bitcast.16, bf16[2,1,576,128]{3,2,1,0:T(8,128)(2,1)} %features.1, s32[2,1,24,128]{3,2,1,0:T(8,128)} %codes_in.1, s32[2,1,128]{2,1,0:T(1,128)} %counts_in.1, ...), custom_call_target="tpu_custom_call" | custom-call | tf_op jit(solution)/shard_map/step/pallas_call | solution.py:579
  44.7 0.6 %copy.17 = f32[2,1,128]{2,1,0:T(1,128)} copy(f32[2,1,128]{2,1,0:T(1,128)S(1)} %get-tuple-element.9) | data formatting | bytes 2048
  45.2 0.6 %copy.18 = f32[2,1,3,128]{3,1,2,0:T(1,128)} copy(f32[2,1,3,128]{3,1,2,0:T(1,128)S(1)} %bitcast.11) | data formatting | bytes 6144
  45.8 0.6 %copy.19 = f32[2,1,3,128]{3,1,2,0:T(1,128)} copy(f32[2,1,3,128]{3,1,2,0:T(1,128)S(1)} %bitcast.10) | data formatting | bytes 6144
